TPU v7x, 512 devices: a whole 4x8x8 slice. The times are simulated.
512 devices in a mesh: dp: 8 (over x, core), ctx: 64 (over y, z).
Axes of the slice: x: 4, y: 8, z: 8, core: 2. Of those that a mesh axis runs over, the one named last changes fastest.
Arguments:
- queries: bfloat16 [8192, 4096], P(('dp', 'ctx')), may hold values from -150 to 150
- keys: bfloat16 [131072, 1024], P(('dp', 'ctx')), may hold values from -8 to 8
- values: bfloat16 [131072, 1024], P(('dp', 'ctx')), may hold values from -6 to 6
- learned_compress_queries: bfloat16 [16, 1024], replicated, may hold values from -150 to 150
- span_len: int32 [8, 64], P('dp', 'ctx'), may hold values from 1 to 16, 768 in all within a row
- span_offset: int32 [8, 64], P('dp', 'ctx'), may hold values from 0 to 240
- destination: int32 [8192, 1], P(('dp', 'ctx')), may hold values from 0 to 63; in each aligned block of 16 rows (0 to 15, 16 to 31, ...) at most 2 rows name the same one
- cotangent: bfloat16 [8192, 4096], P(('dp', 'ctx')), may hold values from -6 to 6
- adapter_a: bfloat16 [64, 16, 4096], P('ctx'), may hold values from -0.09375 to 0.09375
- adapter_b: bfloat16 [64, 16, 4096], P('ctx'), may hold values from -0.09375 to 0.09375
Outputs:
- grad_rows: bfloat16 [8192, 4096], P(('dp', 'ctx'))
- grad_a: float32 [64, 16, 4096], P('ctx')
- grad_b: float32 [64, 16, 4096], P('ctx')
Inputs may be any that keep to these rules, and one draw needn't show every extreme that they name: `destination`: in each device's 16 slots (aligned blocks of rows) no decoder is named more than 2 times, a bound that some block reaches.
All inputs are finite; a program needn't handle non-finite values. No bound on the sum of `span_len` on one device may be relied on, other than what follows from the above.
Results may differ from a plain program's by a relative error of at most 0.025.
Values may be sent and summed in bfloat16 or wider, within the bound.
A program may use at most 64 MiB of HBM per device.

v0:
```python
import math

import jax
import jax.numpy as jnp
from jax import lax
from jax.sharding import PartitionSpec as P

QUERY_HEADS = 32
KEY_VALUE_HEADS = 8
HEAD_SIZE = 128
COMPRESSED_ROWS = 16


SCALE = 2.0
EPS = 1e-06
NEGATIVE_FLOOR = -1e30


def absorb(state, query_matrix, keys_blk, vals_blk, visible):
    count = keys_blk.shape[0]
    heads = query_matrix.shape[1]
    width = query_matrix.shape[3]
    expanded_keys = keys_blk.reshape(count, heads, width)
    expanded_values = vals_blk.reshape(count, heads, width)
    attention_score = jnp.einsum(
        "shgd,nhd->shgn", query_matrix, expanded_keys, preferred_element_type=jnp.float32
    ) * (1.0 / math.sqrt(width))
    seen = visible[:, None, None, :]
    attention_score = jnp.where(seen, attention_score, NEGATIVE_FLOOR)
    peak, total, accum = state
    newpeak = jnp.maximum(peak, jnp.max(attention_score, axis=-1))
    keep = jnp.exp(peak - newpeak)
    prob = jnp.where(seen, jnp.exp(attention_score - newpeak[..., None]), 0.0)
    total = total * keep + jnp.sum(prob, axis=-1)
    accum = accum * keep[..., None] + jnp.einsum(
        "shgn,nhd->shgd",
        prob.astype(jnp.bfloat16),
        expanded_values,
        preferred_element_type=jnp.float32,
    )
    return (newpeak, total, accum)


def absorb_rows(state, query_matrix, keys_blk, vals_blk, visible):
    count = keys_blk.shape[0]
    blocks = count // 256
    kb = keys_blk.reshape(blocks, 256, keys_blk.shape[1])
    vb = vals_blk.reshape(blocks, 256, vals_blk.shape[1])
    mb = visible.reshape(visible.shape[0], blocks, 256).transpose(1, 0, 2)

    def step(current, item):
        return (absorb(current, query_matrix, item[0], item[1], item[2]), None)

    state, _ = lax.scan(step, state, (kb, vb, mb))
    return state


def attend(queries, keys, values, learned_compress_queries, offset, length):
    span_slots = queries.shape[0]
    model = queries.shape[1]
    segment_length = keys.shape[0]
    query_group = QUERY_HEADS // KEY_VALUE_HEADS
    here = lax.axis_index("ctx")
    query_matrix = queries.reshape(span_slots, KEY_VALUE_HEADS, query_group, HEAD_SIZE)
    expanded_keys = keys.reshape(segment_length, KEY_VALUE_HEADS, HEAD_SIZE)
    expanded_values = values.reshape(segment_length, KEY_VALUE_HEADS, HEAD_SIZE)
    compressor_query = learned_compress_queries.reshape(COMPRESSED_ROWS, KEY_VALUE_HEADS, HEAD_SIZE)
    attention_score = jnp.einsum(
        "cpf,ipf->pci", compressor_query, expanded_keys, preferred_element_type=jnp.float32
    ) * (1.0 / math.sqrt(HEAD_SIZE))
    softmax_weight = jax.nn.softmax(attention_score, axis=-1).astype(jnp.bfloat16)
    short_keys = (
        jnp.einsum(
            "wio,owx->iwx", softmax_weight, expanded_keys, preferred_element_type=jnp.float32
        )
        .astype(jnp.bfloat16)
        .reshape(COMPRESSED_ROWS, KEY_VALUE_HEADS * HEAD_SIZE)
    )
    short_vals = (
        jnp.einsum(
            "wio,owx->iwx", softmax_weight, expanded_values, preferred_element_type=jnp.float32
        )
        .astype(jnp.bfloat16)
        .reshape(COMPRESSED_ROWS, KEY_VALUE_HEADS * HEAD_SIZE)
    )
    state = (
        jnp.full((span_slots, KEY_VALUE_HEADS, query_group), NEGATIVE_FLOOR, jnp.float32),
        jnp.zeros((span_slots, KEY_VALUE_HEADS, query_group), jnp.float32),
        jnp.zeros((span_slots, KEY_VALUE_HEADS, query_group, HEAD_SIZE), jnp.float32),
    )
    position = offset + jnp.arange(span_slots, dtype=jnp.int32)
    local = jnp.arange(segment_length, dtype=jnp.int32)[None, :] <= position[:, None]
    state = absorb(state, query_matrix, keys, values, local)
    piece = (
        lax.all_gather(short_keys, "ctx", axis=0, tiled=True),
        lax.all_gather(short_vals, "ctx", axis=0, tiled=True),
    )
    count = piece[0].shape[0]
    source = jnp.arange(count, dtype=jnp.int32) // COMPRESSED_ROWS
    state = absorb_rows(state, query_matrix, piece[0], piece[1], (source < here)[None, :])
    peak, total, accum = state
    out = (accum / total[..., None]).reshape(span_slots, model)
    live = (jnp.arange(span_slots, dtype=jnp.int32) < length)[:, None]
    return jnp.where(live, out, 0.0).astype(jnp.bfloat16)


def shards(
    queries,
    keys,
    values,
    learned_compress_queries,
    span_len,
    span_offset,
    destination,
    cotangent,
    adapter_a,
    adapter_b,
):
    span_slots = queries.shape[0]
    model = queries.shape[1]
    count = lax.axis_size("ctx")
    cap = max(2, (3 * span_slots + 2 * count - 1) // (2 * count))
    offset = span_offset[0, 0]
    length = span_len[0, 0]
    live = (jnp.arange(span_slots, dtype=jnp.int32) < length)[:, None]
    dy = jnp.where(live, cotangent, jnp.zeros_like(cotangent))
    target = destination[:, 0]
    order_idx = jnp.arange(span_slots, dtype=jnp.int32)
    same = target[:, None] == target[None, :]
    before = order_idx[None, :] < order_idx[:, None]
    rank = jnp.sum((same & before).astype(jnp.int32), axis=1)
    slot = target * cap + rank
    place = (jnp.arange(count * cap, dtype=jnp.int32)[:, None] == slot[None, :]).astype(
        jnp.bfloat16
    )

    def packed(row_block):
        return (
            jnp.dot(place, row_block, preferred_element_type=jnp.float32)
            .astype(jnp.bfloat16)
            .reshape(count, cap, model)
        )

    attn = attend(queries, keys, values, learned_compress_queries, offset, length)
    rows_in, dy_in = (
        lax.all_to_all(packed(attn), "ctx", split_axis=0, concat_axis=0, tiled=True),
        lax.all_to_all(packed(dy), "ctx", split_axis=0, concat_axis=0, tiled=True),
    )
    x = rows_in.reshape(count * cap, model).astype(jnp.float32)
    grads_in = dy_in.reshape(count * cap, model)
    rs = lax.rsqrt(jnp.mean(x * x, axis=-1, keepdims=True) + EPS)
    nrm = x * rs
    normed = nrm.astype(jnp.bfloat16)
    down = adapter_a[0]
    upper = adapter_b[0]
    across = (((1,), (1,)), ((), ()))
    along = (((0,), (0,)), ((), ()))
    hid = lax.dot_general(normed, down, across, preferred_element_type=jnp.float32).astype(
        jnp.bfloat16
    )
    back = (
        SCALE * lax.dot_general(grads_in, upper, across, preferred_element_type=jnp.float32)
    ).astype(jnp.bfloat16)
    grad_b = SCALE * lax.dot_general(hid, grads_in, along, preferred_element_type=jnp.float32)
    grad_a = lax.dot_general(back, normed, along, preferred_element_type=jnp.float32)
    dn = jnp.dot(back, down, preferred_element_type=jnp.float32)
    d_rows = (
        grads_in.astype(jnp.float32) + rs * (dn - nrm * jnp.mean(dn * nrm, axis=-1, keepdims=True))
    ).astype(jnp.bfloat16)
    returned = lax.all_to_all(
        d_rows.reshape(count, cap, model), "ctx", split_axis=0, concat_axis=0, tiled=True
    )
    grad_rows = lax.dot_general(
        place, returned.reshape(count * cap, model), along, preferred_element_type=jnp.float32
    ).astype(jnp.bfloat16)
    grad_a, grad_b = (
        lax.psum(grad_a.astype(jnp.bfloat16), "dp").astype(jnp.float32),
        lax.psum(grad_b.astype(jnp.bfloat16), "dp").astype(jnp.float32),
    )
    return (grad_rows, grad_a[None], grad_b[None])


def solution(mesh):
    in_specs = (
        P(("dp", "ctx"), None),
        P(("dp", "ctx"), None),
        P(("dp", "ctx"), None),
        P(),
        P("dp", "ctx"),
        P("dp", "ctx"),
        P(("dp", "ctx"), None),
        P(("dp", "ctx"), None),
        P("ctx", None, None),
        P("ctx", None, None),
    )
    out_specs = (P(("dp", "ctx"), None), P("ctx", None, None), P("ctx", None, None))
    return jax.shard_map(shards, mesh=mesh, in_specs=in_specs, out_specs=out_specs, check_vma=False)
```

profile of v0, /device:TPU:1, one launch (start us, length us, event | category | flops | bytes accessed | tf_op | source)
XLA Modules:
  0.0 355.1 jit_solution(18318135870249494899)
XLA Ops:
  7.2 1.5 fusion.61
  8.8 1.3 fusion.19
  10.1 0.6 copy.103
  10.8 1.3 fusion.20
  12.0 0.6 copy.102
  13.4 0.2 convert_reduce_fusion
  13.6 0.5 convolution_convert_fusion.1
  14.1 1.5 reshape.203
  15.6 17.5 %all-to-all-start = ((bf16[64,2,4096]{2,1,0:T(2,128)(2,1)}), bf16[64,2,4096]{2,1,0:T(2,128)(2,1)}, u32[]{:S(2)}, u32[]{:S(2)}) async-start(bf16[64,2,4096]{2,1,0:T(2,128)(2,1)} %reshape.203), calls=%async_computation | async-start | bytes 2097152 | tf_op jit(solution)/shard_map/all_to_all | solution.py:147
  34.2 0.4 fusion.60
  34.7 0.3 fusion.32
  35.0 0.3 fusion.16
  35.3 79.1 %all-gather.3.cloned.1.call-done = bf16[1024,1024]{1,0:T(8,128)(2,1)} async-done(((bf16[16,1024]{1,0:T(8,128)(2,1)}), bf16[1024,1024]{1,0:T(8,128)(2,1)}) %all-gather.3.cloned.1.call-update) | async-done | bytes 2097168 | tf_op jit(solution)/shard_map/all_gather | solution.py:95
  114.4 84.1 %all-gather.5.cloned.1.call-done = bf16[1024,1024]{1,0:T(8,128)(2,1)} async-done(((bf16[16,1024]{1,0:T(8,128)(2,1)}), bf16[1024,1024]{1,0:T(8,128)(2,1)}) %all-gather.5.cloned.1.call-update) | async-done | bytes 2097168 | tf_op jit(solution)/shard_map/all_gather | solution.py:96
  198.5 11.0 %while.14 = (s32[]{:T(128)}, f32[16,8,4]{0,2,1:T(4,128)S(1)}, f32[16,8,4]{0,2,1:T(4,128)S(1)}, f32[16,8,4,128]{3,0,2,1:T(8,128)S(1)}, pred[4,1,256]{2,1,0:T(4,12...) while((s32[]{:T(128)}, f32[16,8,4]{0,2,1:T(4,128)S(1)}, ...), condition=%wide.region_8.9_spmd, body=%wide.region_5.8_spmd.sunk | while | flops 68420608 | bytes 7505253 | solution.py:54
  198.5 1.3 constant_dynamic-slice_fusion.3
  199.8 0.2 copy.106
  200.0 0.3 fusion.90
  200.4 0.3 fusion.91
  200.7 0.2 copy.107
  200.9 0.4 fusion.92
  201.3 1.3 constant_dynamic-slice_fusion.3
  202.6 0.2 copy.106
  202.8 0.3 fusion.90
  203.1 0.3 fusion.91
  203.4 0.2 copy.107
  203.6 0.4 fusion.92
  204.0 1.3 constant_dynamic-slice_fusion.3
  205.3 0.2 copy.106
  205.6 0.3 fusion.90
  205.9 0.3 fusion.91
  206.2 0.2 copy.107
  206.4 0.4 fusion.92
  206.8 1.3 constant_dynamic-slice_fusion.3
  208.1 0.2 copy.106
  208.3 0.3 fusion.90
  208.6 0.3 fusion.91
  208.9 0.2 copy.107
  209.1 0.4 fusion.92
  209.5 0.1 broadcast_divide_fusion
  209.8 0.5 convolution_convert_fusion
  210.3 1.5 reshape.214
  211.8 8.5 %all-to-all-start.1 = ((bf16[64,2,4096]{2,1,0:T(2,128)(2,1)}), bf16[64,2,4096]{2,1,0:T(2,128)(2,1)S(1)}, u32[]{:S(2)}, u32[]{:S(2)}) async-start(bf16[64,2,4096]{2,1,0:T(2,128)(2,1)} %reshape.214), calls=%async_computation.1 | async-start | bytes 2097152 | tf_op jit(solution)/shard_map/all_to_all | solution.py:146
  220.4 1.5 reshape.204
  221.9 0.4 fusion.21
  222.2 21.0 %all-to-all-done.1 = bf16[64,2,4096]{2,1,0:T(2,128)(2,1)S(1)} async-done(((bf16[64,2,4096]{2,1,0:T(2,128)(2,1)}), bf16[64,2,4096]{2,1,0:T(2,128)(2,1)S(1)}, u32[]{:S(2)}, u32[]{:S(2)}) %all-to-all-start.1) | async-done | bytes 1048608 | tf_op jit(solution)/shard_map/all_to_all | solution.py:146
  243.2 1.2 multiply_reduce_fusion.1
  244.4 0.1 rsqrt.13
  244.5 0.3 reshape.217
  244.9 0.5 multiply_reduce_fusion
  245.4 0.7 copy-done.2
  246.1 1.7 add_convert_fusion
  247.8 2.5 reshape.215
  250.3 13.0 %all-to-all-start.2 = ((bf16[64,2,4096]{2,1,0:T(2,128)(2,1)}), bf16[64,2,4096]{2,1,0:T(2,128)(2,1)}, u32[]{:S(2)}, u32[]{:S(2)}) async-start(bf16[64,2,4096]{2,1,0:T(2,128)(2,1)} %reshape.215), calls=%async_computation.2 | async-start | bytes 2097152 | tf_op jit(solution)/shard_map/all_to_all | solution.py:170
  263.3 0.2 all-reduce.3.cloned.1.call-start
  263.6 2.4 multiply_convert_fusion
  266.0 2.3 convert_element_type.95
  268.3 1.0 fusion.12
  269.3 2.8 fusion.13
  272.1 70.8 %all-reduce.3.cloned.1.call-done = (bf16[1,16,4096]{2,1,0:T(8,128)(2,1)}, bf16[1,16,4096]{2,1,0:T(8,128)(2,1)}) async-done(((bf16[1,16,4096]{2,1,0:T(8,128)(2,1)}, bf16[1,16,4096]{2,1,0:T(8,128)(2,1)}), (bf16[1,16,4096]{2,1,0:T(8,128)(2,1)}, bf16[1,16,4096]{2,1,0:T(8,128)(2,1)})) %all-reduce.3.cloned.1.call-update) | async-done | bytes 262160 | tf_op jit(solution)/shard_map/psum | solution.py:177
  342.9 1.6 broadcast_in_dim.108
  344.5 1.6 broadcast_in_dim.110
  346.1 1.5 reshape.216
  347.6 1.0 convolution_convert_fusion.3
  (57 shorter events, 1.0 us)
Async XLA Ops:
  7.2 237.7 %copy-start = (bf16[1,16,4096]{2,1,0:T(8,128)(2,1)S(1)}, bf16[1,16,4096]{2,1,0:T(8,128)(2,1)}, u32[]{:S(2)}) copy-start(bf16[1,16,4096]{2,1,0:T(8,128)(2,1)} %param.20) | copy-start | bytes 393220
  7.2 6.2 %copy-start.9 = (s32[16,1]{0,1:T(1,128)S(1)}, s32[16,1]{0,1:T(1,128)}, u32[]{:S(2)}) copy-start(s32[16,1]{0,1:T(1,128)} %param.18) | copy-start | bytes 196
  7.2 6.4 %copy-start.8 = (bf16[16,4096]{1,0:T(8,128)(2,1)S(1)}, bf16[16,4096]{1,0:T(8,128)(2,1)}, u32[]{:S(2)}) copy-start(bf16[16,4096]{1,0:T(8,128)(2,1)} %param.19) | copy-start | bytes 393220
  7.2 107.2 %all-gather.3.cloned.1.call-start = ((), (), s32[]{:S(2)}) async-start(), calls=%async_computation.3 | async-start | bytes 2129920 | tf_op jit(solution)/shard_map/all_gather | solution.py:95
  10.7 187.8 %all-gather.5.cloned.1.call-start = ((), (), s32[]{:S(2)}) async-start(), calls=%async_computation.4 | async-start | bytes 2129920 | tf_op jit(solution)/shard_map/all_gather | solution.py:96
  14.0 19.7 %copy-start.7 = (bf16[16,4096]{1,0:T(8,128)(2,1)S(1)}, bf16[16,4096]{1,0:T(8,128)(2,1)}, u32[]{:S(2)}) copy-start(bf16[16,4096]{1,0:T(8,128)(2,1)} %param.12) | copy-start | bytes 393220
  14.1 19.8 %copy-start.4 = (bf16[256,1024]{1,0:T(8,128)(2,1)S(1)}, bf16[256,1024]{1,0:T(8,128)(2,1)}, u32[]{:S(2)}) copy-start(bf16[256,1024]{1,0:T(8,128)(2,1)} %param.13) | copy-start | bytes 1572868
  15.6 18.4 %copy-start.5 = (bf16[256,1024]{1,0:T(8,128)(2,1)S(1)}, bf16[256,1024]{1,0:T(8,128)(2,1)}, u32[]{:S(2)}) copy-start(bf16[256,1024]{1,0:T(8,128)(2,1)} %param.14) | copy-start | bytes 1572868
  15.6 196.3 %all-to-all-start = ((bf16[64,2,4096]{2,1,0:T(2,128)(2,1)}), bf16[64,2,4096]{2,1,0:T(2,128)(2,1)}, u32[]{:S(2)}, u32[]{:S(2)}) async-start(bf16[64,2,4096]{2,1,0:T(2,128)(2,1)} %reshape.203), calls=%async_computation | async-start | bytes 2097152 | tf_op jit(solution)/shard_map/all_to_all | solution.py:147
  211.8 10.0 %copy-start.6 = (bf16[1,16,4096]{2,1,0:T(8,128)(2,1)S(1)}, bf16[1,16,4096]{2,1,0:T(8,128)(2,1)}, u32[]{:S(2)}) copy-start(bf16[1,16,4096]{2,1,0:T(8,128)(2,1)} %param.21) | copy-start | bytes 393220
  211.8 31.4 %all-to-all-start.1 = ((bf16[64,2,4096]{2,1,0:T(2,128)(2,1)}), bf16[64,2,4096]{2,1,0:T(2,128)(2,1)S(1)}, u32[]{:S(2)}, u32[]{:S(2)}) async-start(bf16[64,2,4096]{2,1,0:T(2,128)(2,1)} %reshape.214), calls=%async_computation.1 | async-start | bytes 2097152 | tf_op jit(solution)/shard_map/all_to_all | solution.py:146
  221.8 22.5 %copy-start.1 = (bf16[128,4096]{1,0:T(8,128)(2,1)}, bf16[128,4096]{1,0:T(8,128)(2,1)S(1)}, u32[]{:S(2)}) copy-start(bf16[128,4096]{1,0:T(8,128)(2,1)S(1)} %reshape.204) | copy-start | bytes 3145732
  244.9 1.2 copy-start.2
  250.3 95.8 %all-to-all-start.2 = ((bf16[64,2,4096]{2,1,0:T(2,128)(2,1)}), bf16[64,2,4096]{2,1,0:T(2,128)(2,1)}, u32[]{:S(2)}, u32[]{:S(2)}) async-start(bf16[64,2,4096]{2,1,0:T(2,128)(2,1)} %reshape.215), calls=%async_computation.2 | async-start | bytes 2097152 | tf_op jit(solution)/shard_map/all_to_all | solution.py:170
  263.3 79.6 %all-reduce.3.cloned.1.call-start = ((), (), s32[]{:S(2)}) async-start(), calls=%async_computation.5 | async-start | bytes 524288 | tf_op jit(solution)/shard_map/psum | solution.py:177
  266.0 3.3 copy-start.3
Sparse Core Ops, SparseCore 0:
  11.6 102.7 all-gather.2
  118.0 80.5 all-gather.4
  272.2 70.6 all-reduce.2
where the time goes:
time: 356 us; the launch traced here: 355 us
  waiting for transfers between devices  255 us (72%)
  starting transfers between devices  39.4 us (11%)
  local copies, waits for them, and re-layouts  20.5 us (6%)
  between operations  15.3 us (4%)
  matrix products  14 us (4%)
  other arithmetic  10.5 us (3%)
    all_gather x1, waiting for transfers between devices, attend(): lax.all_gather(short_vals, 'ctx', axis=0, tiled=True)  84.1 us
    all_gather x1, waiting for transfers between devices, attend(): lax.all_gather(short_keys, 'ctx', axis=0, tiled=True)  79.1 us
    psum x1, waiting for transfers between devices, shards(): lax.psum(grad_a.astype(jnp.bfloat16), 'dp').astype(jnp.float32)  70.8 us
    all_to_all x1, waiting for transfers between devices, shards(): lax.all_to_all(packed(attn), 'ctx', split_axis=0, concat_axis=0, tiled=True)  21 us
    all_to_all x1, starting transfers between devices, shards(): lax.all_to_all(packed(dy), 'ctx', split_axis=0, concat_axis=0, tiled=True)  17.5 us
    all_to_all x1, starting transfers between devices, shards(): lax.all_to_all(d_rows.reshape(count, cap, model), 'ctx', split_axis=0, co...  13 us
    all_to_all x1, starting transfers between devices, shards(): lax.all_to_all(packed(attn), 'ctx', split_axis=0, concat_axis=0, tiled=True)  8.53 us
  transfers between devices with their start and end apart: 6, of which 4 were waited for; matrix products, arithmetic and copies ran while one was open for 9% of the time, Pallas kernels for 0%

commit v1 on v0

v1 whole, which is shorter than its diff:
```python
import functools
import math

import jax
import jax.numpy as jnp
from jax import lax
from jax.experimental import pallas as pl
from jax.experimental.pallas import tpu as pltpu
from jax.sharding import Mesh
from jax.sharding import PartitionSpec as P

QUERY_HEADS = 32
KEY_VALUE_HEADS = 8
GROUP = QUERY_HEADS // KEY_VALUE_HEADS
HEAD_SIZE = 128
COMPRESSED_ROWS = 16
RANK = 16
SLOTS = 16

SCALE = 2.0
EPS = 1e-06
NEGATIVE_FLOOR = -1e30
SOFTMAX_SCALE = 1.0 / math.sqrt(HEAD_SIZE)
HIGH = lax.Precision.HIGHEST


def routes(kind, sizes, me):
    dp, y, z = me
    ndp, ny, nz = sizes
    if kind == "plane":
        def route(i):
            yy, zz = i // nz, i % nz
            return {"dp": dp, "y": yy, "z": zz}, zz
        return ny * nz, route, y * nz + z
    if kind == "owners":
        def route(i):
            pp, zz = i // nz, i % nz
            return {"dp": pp, "y": dp, "z": zz}, zz
        return ndp * nz, route, y * nz + z
    axis, form = kind.split("_")
    n = {"dp": ndp, "y": ny, "z": nz}[axis]
    own = {"dp": dp, "y": y, "z": z}[axis]

    def route(i):
        where = {"dp": dp, "y": y, "z": z}
        where[axis] = i
        return where, (i if form == "swap" else None)

    return n, route, own


def exchange_kernel(kinds, sizes, *refs):
    n_items = len(kinds)
    ins, outs = refs[:n_items], refs[n_items : 2 * n_items]
    sems = refs[2 * n_items :]
    me = (lax.axis_index("dp"), lax.axis_index("y"), lax.axis_index("z"))
    dp, y, z = me
    ndp, ny, nz = sizes
    barrier = pltpu.get_barrier_semaphore()
    owners = "owners" in kinds

    greeted = []
    if "plane" in kinds:
        greeted.append("plane")
    for axis in ("z", "y", "dp"):
        if any(kind.startswith(axis + "_") for kind in kinds):
            if not (axis in ("y", "z") and "plane" in kinds):
                greeted.append(axis + "_spread")
    expected = 0
    for kind in greeted:
        n, route, own = routes(kind, sizes, me)

        def greet(step, carry, n=n, route=route, own=own):
            device, _ = route(lax.rem(own + step, n))
            pl.semaphore_signal(
                barrier, inc=1, device_id=device, device_id_type=pl.DeviceIdType.MESH
            )
            return carry

        lax.fori_loop(1, n, greet, 0)
        expected += n - 1
    if owners:
        mine = dp == y

        def greet_sender(i, carry):
            yy, zz = i // nz, lax.rem(i, nz)

            @pl.when(jnp.logical_not(mine & (yy == y) & (zz == z)))
            def _():
                pl.semaphore_signal(
                    barrier,
                    inc=1,
                    device_id={"dp": y, "y": yy, "z": zz},
                    device_id_type=pl.DeviceIdType.MESH,
                )

            return carry

        lax.fori_loop(0, ny * nz, greet_sender, 0)
        pl.semaphore_wait(barrier, ndp * nz - mine.astype(jnp.int32))
    if expected:
        pl.semaphore_wait(barrier, expected)

    def remote(item, i):
        kind = kinds[item]
        n, route, own = routes(kind, sizes, me)
        device, block = route(i)
        src = ins[item] if block is None else ins[item].at[block]
        return pltpu.make_async_remote_copy(
            src_ref=src,
            dst_ref=outs[item].at[own],
            send_sem=sems[3 * item].at[i],
            recv_sem=sems[3 * item + 1].at[own],
            device_id=device,
            device_id_type=pl.DeviceIdType.MESH,
        )

    def arrival(item, i):
        kind = kinds[item]
        block = None if kind.endswith("spread") else 0
        src = ins[item] if block is None else ins[item].at[block]
        return pltpu.make_async_remote_copy(
            src_ref=src,
            dst_ref=outs[item].at[i],
            send_sem=sems[3 * item].at[i],
            recv_sem=sems[3 * item + 1].at[i],
            device_id={"dp": dp, "y": y, "z": z},
            device_id_type=pl.DeviceIdType.MESH,
        )

    def local(item):
        kind = kinds[item]
        n, route, own = routes(kind, sizes, me)
        if kind in ("plane", "owners"):
            block = z
        else:
            block = own if kind.endswith("swap") else None
        src = ins[item] if block is None else ins[item].at[block]
        return pltpu.make_async_copy(src, outs[item].at[own], sems[3 * item + 2])

    for item, kind in enumerate(kinds):
        n, route, own = routes(kind, sizes, me)
        if kind == "owners":
            def send(i, carry, item=item):
                self_here = mine & (i == dp * nz + z)

                @pl.when(self_here)
                def _():
                    local(item).start()

                @pl.when(jnp.logical_not(self_here))
                def _():
                    remote(item, i).start()

                return carry

            lax.fori_loop(0, n, send, 0)
        else:
            def send(step, carry, item=item, n=n, own=own):
                remote(item, lax.rem(own + step, n)).start()
                return carry

            lax.fori_loop(1, n, send, 0)
            local(item).start()

    for item, kind in enumerate(kinds):
        n, route, own = routes(kind, sizes, me)
        if kind == "owners":
            def finish(i, carry, item=item):
                @pl.when(jnp.logical_not(mine & (i == dp * nz + z)))
                def _():
                    remote(item, i).wait_send()

                return carry

            lax.fori_loop(0, n, finish, 0)

            def collect(i, carry, item=item):
                @pl.when(jnp.logical_not(mine & (i == y * nz + z)))
                def _():
                    arrival(item, i).wait_recv()

                return carry

            lax.fori_loop(0, ny * nz, collect, 0)

            @pl.when(mine)
            def _(item=item):
                local(item).wait()
        else:
            def finish(step, carry, item=item, n=n, own=own):
                peer = lax.rem(own + step, n)
                remote(item, peer).wait_send()
                arrival(item, peer).wait_recv()
                return carry

            lax.fori_loop(1, n, finish, 0)
            local(item).wait()


def exchange(name, collective_id, sizes, *items):
    arrays = [item[0] for item in items]
    kinds = tuple(item[1] for item in items)
    ndp, ny, nz = sizes
    shapes, scratch = [], []
    for array, kind in zip(arrays, kinds):
        if kind in ("plane", "owners"):
            senders, targets = ny * nz, (ny * nz if kind == "plane" else ndp * nz)
            block = array.shape[1:]
        else:
            senders = targets = {"dp": ndp, "y": ny, "z": nz}[kind.split("_")[0]]
            block = array.shape[1:] if kind.endswith("swap") else array.shape
        shapes.append(jax.ShapeDtypeStruct((senders,) + block, array.dtype))
        scratch += [
            pltpu.SemaphoreType.DMA((targets,)),
            pltpu.SemaphoreType.DMA((senders,)),
            pltpu.SemaphoreType.DMA(()),
        ]
    return pl.pallas_call(
        functools.partial(exchange_kernel, kinds, sizes),
        out_shape=shapes,
        in_specs=[pl.BlockSpec(memory_space=pltpu.VMEM)] * len(arrays),
        out_specs=[pl.BlockSpec(memory_space=pltpu.VMEM)] * len(arrays),
        scratch_shapes=scratch,
        compiler_params=pltpu.CompilerParams(
            collective_id=collective_id, has_side_effects=True
        ),
        name=name,
    )(*arrays)


def compress(keys, values, learned):
    tokens = keys.shape[0]
    k = keys.reshape(tokens, KEY_VALUE_HEADS, HEAD_SIZE)
    v = values.reshape(tokens, KEY_VALUE_HEADS, HEAD_SIZE)
    c = learned.reshape(COMPRESSED_ROWS, KEY_VALUE_HEADS, HEAD_SIZE)
    score = jnp.einsum("cpf,ipf->pci", c, k, preferred_element_type=jnp.float32) * SOFTMAX_SCALE
    weight = jax.nn.softmax(score, axis=-1).astype(jnp.bfloat16)
    short = lambda rows: jnp.einsum(
        "wio,owx->wix", weight, rows, preferred_element_type=jnp.float32
    ).astype(jnp.bfloat16)
    return short(k), short(v)


def attend_local(queries, keys, values, offset):
    slots, tokens = queries.shape[0], keys.shape[0]
    q = queries.reshape(slots, KEY_VALUE_HEADS, GROUP, HEAD_SIZE)
    k = keys.reshape(tokens, KEY_VALUE_HEADS, HEAD_SIZE)
    v = values.reshape(tokens, KEY_VALUE_HEADS, HEAD_SIZE)
    score = jnp.einsum("shgd,nhd->hsgn", q, k, preferred_element_type=jnp.float32) * SOFTMAX_SCALE
    position = offset + jnp.arange(slots, dtype=jnp.int32)
    seen = jnp.arange(tokens, dtype=jnp.int32)[None, :] <= position[:, None]
    seen = seen[None, :, None, :]
    score = jnp.where(seen, score, NEGATIVE_FLOOR)
    peak = jnp.max(score, axis=-1)
    prob = jnp.where(seen, jnp.exp(score - peak[..., None]), 0.0)
    total = jnp.sum(prob, axis=-1)
    acc = jnp.einsum(
        "hsgn,nhd->hsgd", prob.astype(jnp.bfloat16), v, preferred_element_type=jnp.float32
    )
    out = (acc / total[..., None]).astype(jnp.bfloat16)
    return out.reshape(KEY_VALUE_HEADS, slots, GROUP * HEAD_SIZE), peak + jnp.log(total)


def shards(sizes, queries, keys, values, learned, span_len, span_offset, destination, cotangent,
           adapter_a, adapter_b):
    ndp, ny, nz = sizes
    decoders = ny * nz
    model = queries.shape[1]
    wide = model // nz
    narrow = wide // ny
    share = RANK // ndp
    rows = nz * SLOTS
    dp, y = lax.axis_index("dp"), lax.axis_index("y")
    swap = functools.partial(jnp.einsum, "shd->hsd")

    live = (jnp.arange(SLOTS, dtype=jnp.int32) < span_len[0, 0])[:, None]
    dy = jnp.where(live, cotangent, jnp.zeros_like(cotangent))
    ck, cv = compress(keys, values, learned)
    out_local, lse = attend_local(queries, keys, values, span_offset[0, 0])
    by_head = lambda array: array.reshape(SLOTS, nz, wide).transpose(1, 0, 2)
    packet = jnp.concatenate([by_head(queries), by_head(dy), out_local, ck, cv], axis=-1)
    facts = jnp.concatenate([destination.astype(jnp.float32), live.astype(jnp.float32)], axis=1)
    facts = jnp.concatenate([lse, jnp.broadcast_to(facts[None], (nz, SLOTS, 2))], axis=-1)
    facts = jnp.pad(facts, ((0, 0), (0, 0), (0, 128 - facts.shape[-1])))
    part = lambda adapter: lax.dynamic_slice_in_dim(adapter[0], dp * share, share, 0).reshape(
        share, nz, wide
    ).transpose(1, 0, 2)
    adapters = jnp.concatenate([part(adapter_a), part(adapter_b)], axis=1)

    packet, facts, adapters = exchange(
        "heads", 1, sizes, (packet, "z_swap"), (facts, "z_swap"), (adapters, "plane")
    )
    packet = packet.reshape(rows, -1)
    facts = facts.reshape(rows, -1)
    q, dy, out_local = packet[:, :wide], packet[:, wide : 2 * wide], packet[:, 2 * wide : 3 * wide]
    short, adapters = exchange(
        "short", 2, sizes, (packet[:, 3 * wide :], "y_spread"), (adapters, "dp_spread")
    )
    short = short.reshape(ny * rows, 2 * HEAD_SIZE)
    ck, cv = short[:, :HEAD_SIZE], short[:, HEAD_SIZE:]
    lse, target, live = facts[:, :GROUP], facts[:, GROUP : GROUP + 1], facts[:, GROUP + 1 : GROUP + 2]

    heads = q.reshape(rows, GROUP, HEAD_SIZE)
    score = jnp.einsum("rgd,kd->grk", heads, ck, preferred_element_type=jnp.float32) * SOFTMAX_SCALE
    segment = y * nz + jnp.arange(rows, dtype=jnp.int32) // SLOTS
    source = jnp.arange(ny * rows, dtype=jnp.int32) // COMPRESSED_ROWS
    seen = (source[None, :] < segment[:, None])[None]
    score = jnp.where(seen, score, NEGATIVE_FLOOR)
    lse = lse.T
    peak = jnp.maximum(lse, jnp.max(score, axis=-1))
    prob = jnp.where(seen, jnp.exp(score - peak[..., None]), 0.0)
    weight = jnp.exp(lse - peak)
    total = weight + jnp.sum(prob, axis=-1)
    acc = jnp.einsum(
        "grk,kd->grd", prob.astype(jnp.bfloat16), cv, preferred_element_type=jnp.float32
    )
    home = out_local.reshape(rows, GROUP, HEAD_SIZE).transpose(1, 0, 2).astype(jnp.float32)
    attn = (acc + weight[..., None] * home) / total[..., None]
    attn = attn.transpose(1, 0, 2).reshape(rows, wide)
    attn = jnp.where(live > 0.5, attn, 0.0).astype(jnp.bfloat16)

    adapters = adapters.reshape(ndp, decoders, 2, share, wide)
    downs = adapters[:, :, 0].reshape(ndp * decoders * share, wide)
    ups = adapters[:, :, 1].reshape(ndp * decoders * share, wide)
    column = jnp.arange(ndp * decoders * share, dtype=jnp.int32)
    column_decoder = (column // share) % decoders
    column_rank = column // (share * decoders) * share + column % share
    own = target.astype(jnp.int32) == column_decoder[None, :]
    pick = column_rank[:, None] == jnp.arange(RANK, dtype=jnp.int32)[None, :]
    across = (((1,), (1,)), ((), ()))

    def narrowed(left, right):
        full = lax.dot_general(left, right, across, preferred_element_type=jnp.float32)
        return lax.dot_general(
            pick.astype(jnp.float32), jnp.where(own, full, 0.0), (((0,), (1,)), ((), ())),
            precision=HIGH, preferred_element_type=jnp.float32,
        )

    x = attn.astype(jnp.float32)
    square = jnp.sum(x * x, axis=1)[None]
    partial = jnp.concatenate(
        [narrowed(attn, downs), narrowed(dy, ups), square, jnp.zeros((7, rows), jnp.float32)], axis=0
    )
    (partial,) = exchange("sums", 3, sizes, (partial, "z_spread"))
    sums = jnp.sum(partial, axis=0)
    rs = lax.rsqrt(sums[2 * RANK : 2 * RANK + 1] / model + EPS)
    hid_exact = sums[:RANK] * rs
    hid = hid_exact.astype(jnp.bfloat16)
    back = (SCALE * sums[RANK : 2 * RANK]).astype(jnp.bfloat16)
    dot_mean = jnp.sum(back.astype(jnp.float32) * hid_exact, axis=0, keepdims=True) / model
    rs_column, mean_column = rs.T, dot_mean.T
    spread = lax.dot_general(
        back, pick.astype(jnp.bfloat16), (((0,), (1,)), ((), ())), preferred_element_type=jnp.float32
    )
    spread = jnp.where(own, spread, 0.0).astype(jnp.bfloat16)
    dn = jnp.dot(spread, downs, preferred_element_type=jnp.float32)
    nrm = x * rs_column
    d_rows = (dy.astype(jnp.float32) + rs_column * (dn - nrm * mean_column)).astype(jnp.bfloat16)
    normed = nrm.astype(jnp.bfloat16)

    slices = lambda array: array.reshape(rows, ny, narrow).transpose(1, 0, 2)
    columns = jnp.concatenate([slices(normed), slices(dy)], axis=-1)
    small = jnp.concatenate(
        [hid, back, jnp.broadcast_to(target.T, (RANK, rows)).astype(jnp.bfloat16)], axis=0
    )
    d_rows, columns, small = exchange(
        "rows", 4, sizes,
        (d_rows.reshape(nz, SLOTS, wide), "z_swap"), (columns, "y_swap"), (small, "y_spread"),
    )
    grad_rows = d_rows.transpose(1, 0, 2).reshape(SLOTS, model)
    columns = columns.reshape(ny * rows, 2 * narrow)
    small = small.transpose(1, 0, 2).reshape(3 * RANK, ny * rows)
    chosen = (
        small[2 * RANK].astype(jnp.int32)[None, :]
        == jnp.arange(decoders, dtype=jnp.int32)[:, None]
    )[:, None, :]

    def gathered(values_):
        left = jnp.where(chosen, values_[None], jnp.zeros((), jnp.bfloat16))
        return jnp.dot(
            left.reshape(decoders * RANK, ny * rows), columns, preferred_element_type=jnp.float32
        )

    from_hid = SCALE * gathered(small[:RANK])
    from_back = gathered(small[RANK : 2 * RANK])
    is_a = (jnp.arange(2 * narrow, dtype=jnp.int32) < narrow)[None, :]
    terms = jnp.where(is_a, from_back, from_hid).astype(jnp.bfloat16)
    (terms,) = exchange(
        "terms", 5, sizes, (terms.reshape(ny, nz * RANK, 2 * narrow), "dp_swap")
    )
    terms = jnp.sum(terms.astype(jnp.float32), axis=0).astype(jnp.bfloat16)
    (grads,) = exchange("owners", 6, sizes, (terms.reshape(nz, RANK, 2 * narrow), "owners"))
    grads = grads.reshape(ny, nz, RANK, 2, narrow).transpose(3, 2, 1, 0, 4).astype(jnp.float32)
    grads = grads.reshape(2, 1, RANK, model)
    return grad_rows, grads[0], grads[1]


def solution(mesh):
    ndp, nctx = mesh.devices.shape
    nz = KEY_VALUE_HEADS
    sizes = (ndp, nctx // nz, nz)
    fine = Mesh(mesh.devices.reshape(sizes), ("dp", "y", "z"))
    ctx = ("y", "z")
    both = ("dp", "y", "z")
    in_specs = (
        P(both, None),
        P(both, None),
        P(both, None),
        P(),
        P("dp", ctx),
        P("dp", ctx),
        P(both, None),
        P(both, None),
        P(ctx, None, None),
        P(ctx, None, None),
    )
    out_specs = (P(both, None), P(ctx, None, None), P(ctx, None, None))
    return jax.shard_map(
        functools.partial(shards, sizes), mesh=fine, in_specs=in_specs, out_specs=out_specs,
        check_vma=False,
    )
```

time: 356 us -> 198 us (0.56)
  waiting for transfers between devices: 255 us -> 0 us
  Pallas kernels: 0 us -> 148 us
  starting transfers between devices: 39.4 us -> 0 us
  between operations: 15.3 us -> 2.52 us
    all_gather x2 -> x0, waiting for transfers between devices: 163 us -> none  [the longest x1 84.1 us: attend(): lax.all_gather(short_vals, 'ctx', axis=0, tiled=True)]
    pallas_call x0 -> x6, Pallas kernels: none -> 148 us  [exchange(): pl.pallas_call(functools.partial(exchange_kernel, kinds, sizes), out_shap...]
    psum x1 -> x0, waiting for transfers between devices: 70.8 us -> none  [shards(): lax.psum(grad_a.astype(jnp.bfloat16), 'dp').astype(jnp.float32)]
    all_to_all x3 -> x0, starting transfers between devices: 39.1 us -> none  [the longest x1 17.5 us: shards(): lax.all_to_all(packed(dy), 'ctx', split_axis=0, concat_axis=0, tiled=True)]
    all_to_all x3 -> x0, waiting for transfers between devices: 21 us -> none  [the longest x1 21 us: shards(): lax.all_to_all(packed(attn), 'ctx', split_axis=0, concat_axis=0, tiled=True)]
    dynamic_slice x16 -> x1, local copies, waits for them, and re-layouts: 6.83 us -> 1.06 us  [shards(): lax.dynamic_slice_in_dim(adapter[0], dp * share, share, 0)]
    slice x0 -> x7, local copies, waits for them, and re-layouts: none -> 5.54 us  [the longest x1 2.29 us: shards(): ups = adapters[:, :, 1].reshape(ndp * decoders * share, wide)]
    reshape x10 -> x6, local copies, waits for them, and re-layouts: 9.92 us -> 6.47 us  [the longest x1 4.36 us: shards(): adapters = adapters.reshape(ndp, decoders, 2, share, wide)]
  transfers between devices with their start and end apart: 6 -> 0, of which waited for: 4 -> 0; matrix products, arithmetic and copies ran while one was open for 9% -> 0% of each run, Pallas kernels for 0% -> 0%
where the time goes in v1:
time: 198 us; the launch traced here: 195 us
  Pallas kernels  148 us (75%)
  local copies, waits for them, and re-layouts  21.8 us (11%)
  matrix products  12.4 us (6%)
  other arithmetic  10.1 us (5%)
  between operations  2.52 us (1%)
    pallas_call x6, Pallas kernels, exchange(): pl.pallas_call(functools.partial(exchange_kernel, kinds, sizes), out_shap...  148 us
    reshape x1, local copies, waits for them, and re-layouts, shards(): adapters = adapters.reshape(ndp, decoders, 2, share, wide)  4.36 us

profile of v1, /device:TPU:1, one launch (start us, length us, event | category | flops | bytes accessed | tf_op | source)
XLA Modules:
  0.0 194.8 jit_solution(3952065197345213718)
XLA Ops:
  1.4 1.1 copy.178
  2.6 1.0 reshape.326
  3.6 0.4 fusion.93
  4.0 0.3 fusion.35
  4.3 0.1 copy.179
  4.4 0.3 fusion.16
  5.4 0.1 broadcast_select_fusion.2
  5.6 0.2 convolution_multiply_fusion.2
  5.8 0.2 fusion.94
  6.0 0.3 fusion.19
  6.3 0.3 fusion.18.refs_0_
  6.6 1.1 constant_dynamic-slice_fusion
  7.7 0.7 pad_maximum_fusion.1.refs_2_
  8.3 0.1 copy.136
  8.5 0.1 copy.135
  8.7 0.1 copy.137
  8.8 0.7 select_maximum_fusion.refs_1_
  9.5 40.0 %heads.1 = (bf16[8,16,1792]{2,1,0:T(8,128)(2,1)}, f32[8,16,128]{2,1,0:T(8,128)}, bf16[64,4,512]{2,1,0:T(4,128)(2,1)}) custom-call(bf16[8,16,1792]{2,1,0:T(8,128)(2,1)} %copy-done.2, f32[8,16,128]{2,1,0:T(8,128)} %select_maximum_fusion.refs_1_, bf16[8,4,512]{2,1,0:T(4,128)(2,1)} %pad_maximum_fusion.1.refs_2_), custom_call_target="tpu_custom_call" | custom-call | tf_op jit(solution)/shard_map/heads/pallas_call | solution.py:219
  49.4 1.5 slice.84.refs_0_
  51.0 31.7 %short.1 = (bf16[8,128,256]{2,1,0:T(8,128)(2,1)}, bf16[8,64,4,512]{3,2,1,0:T(4,128)(2,1)}) custom-call(bf16[128,256]{1,0:T(8,128)(2,1)} %slice.84.refs_0_, bf16[64,4,512]{2,1,0:T(4,128)(2,1)} %get-tuple-element.13.refs_1_), custom_call_target="tpu_custom_call" | custom-call | tf_op jit(solution)/shard_map/short/pallas_call | solution.py:219
  82.6 1.1 fusion.92
  83.7 0.2 broadcast_compare_fusion
  83.9 1.4 fusion.1
  85.4 0.5 fusion.2
  86.0 0.1 copy.163
  86.1 0.1 slice_compare_fusion
  86.3 2.3 %multiply_reduce_fusion = (f32[128]{0:T(128)S(1)}, bf16[128,4,128]{0,2,1:T(8,128)(2,1)}, bf16[128,4,128]{0,2,1:T(8,128)(2,1)S(1)}) fusion(pred[128]{0:T(512)(128)(4,1)S(1)} %bitcast.204, f32[128,4]{0,1:T(4,128)S(1)} %get-tuple-element.23, f32[128,4,128]{0,2,1:T(8,128)S(1)} %bitcast.190, f32[128,4]{0,1:T(4,128)S(1)} %get-tuple-element.24, ...), kind=kOutput, calls=%fused_computation.64 | convolution fusion | flops 137363328 | bytes 3021440 | tf_op jit(solution)/shard_map/grk,kd->grd/dot_general | solution.py:315
  88.5 4.4 %reshape.337 = bf16[8,64,2,2,512]{4,3,2,1,0:T(2,128)(2,1)S(1)} reshape(bf16[8,64,4,512]{3,2,1,0:T(4,128)(2,1)} %get-tuple-element.15) | data formatting | bytes 4194304 | tf_op jit(solution)/shard_map/reshape | solution.py:323
  92.9 2.3 %fusion.90 = (bf16[8,64,1,2,512]{4,3,2,1,0:T(2,128)(2,1)S(1)}, bf16[8,64,1,2,512]{4,3,2,1,0:T(2,128)(2,1)}) fusion(bf16[8,64,2,2,512]{4,3,2,1,0:T(2,128)(2,1)S(1)} %reshape.337), kind=kLoop, calls=%fused_computation.163 | loop fusion | bytes 4194304 | tf_op jit(solution)/shard_map/slice | solution.py:325
  95.2 1.5 reshape_squeeze.6
  96.9 0.5 convolution_select_fusion.3
  97.4 0.6 fusion.39
  98.0 0.5 reshape_squeeze.7
  98.4 1.4 convolution_select_fusion.2
  99.8 0.6 fusion.37
  100.4 0.1 pad.13.clone
  100.5 0.7 maximum_maximum_fusion.refs_0_
  101.2 10.6 %sums.1 = f32[8,40,128]{2,1,0:T(8,128)} custom-call(f32[40,128]{1,0:T(8,128)} %maximum_maximum_fusion.refs_0_), custom_call_target="tpu_custom_call" | custom-call | tf_op jit(solution)/shard_map/sums/pallas_call | solution.py:219
  111.8 0.9 reduce_sum.73
  112.8 0.6 pad_maximum_fusion.2.refs_2_
  113.4 0.2 copy.146
  113.6 0.2 fusion.42
  113.8 0.1 copy.147
  113.9 0.2 copy.148
  114.1 0.9 pad_maximum_fusion.refs_1_
  115.0 0.1 copy.164
  115.1 2.1 %fusion.13 = bf16[128,512]{1,0:T(8,128)(2,1)} fusion(bf16[1024,512]{1,0:T(8,128)(2,1)S(1)} %reshape_squeeze.6, bf16[16,128]{1,0:T(8,128)(2,1)S(1)} %get-tuple-element.20, s32[1024]{0:T(1024)S(1)} %get-tuple-element.46, s32[1024]{0:T(1024)S(1)} %get-tuple-element.47, s32[128]{0:T(128)S(1)} %get-tuple-element.38, bf16[128,512]{1,0:T(8,128)(2,1)S(1)} %copy.164, ...), kind=kOutput, calls=%fused_computation.25 | convolution fusion | flops 139411456 | bytes 1455744 | tf_op jit(solution)/shard_map/dot_general | solution.py:357
  117.2 16.9 %rows.1 = (bf16[8,16,512]{2,1,0:T(8,128)(2,1)}, bf16[8,128,128]{2,1,0:T(8,128)(2,1)}, bf16[8,48,128]{2,1,0:T(8,128)(2,1)}) custom-call(bf16[8,16,512]{2,1,0:T(8,128)(2,1)} %bitcast.195, bf16[8,128,128]{2,1,0:T(8,128)(2,1)} %pad_maximum_fusion.refs_1_, bf16[48,128]{1,0:T(8,128)(2,1)} %pad_maximum_fusion.2.refs_2_), custom_call_target="tpu_custom_call" | custom-call | tf_op jit(solution)/shard_map/rows/pallas_call | solution.py:219
  134.1 0.8 slice_bitcast_fusion.6
  134.9 0.7 slice_convert_fusion.1
  135.7 0.4 broadcast_select_fusion.1
  136.1 0.6 copy-done.9
  136.7 0.7 convolution_multiply_fusion
  137.4 1.4 fusion.6
  138.8 9.9 %terms.1 = bf16[8,128,128]{2,1,0:T(8,128)(2,1)} custom-call(bf16[8,128,128]{2,1,0:T(8,128)(2,1)} %bitcast.191), custom_call_target="tpu_custom_call" | custom-call | tf_op jit(solution)/shard_map/terms/pallas_call | solution.py:219
  148.8 1.6 reduce_sum.75
  150.4 38.9 %owners.1 = bf16[64,16,128]{2,1,0:T(8,128)(2,1)} custom-call(bf16[8,16,128]{2,1,0:T(8,128)(2,1)} %bitcast.196), custom_call_target="tpu_custom_call" | custom-call | tf_op jit(solution)/shard_map/owners/pallas_call | solution.py:219
  189.3 1.5 reshape.348
  190.8 0.9 fusion.91
  191.8 0.3 copy.152
  192.1 0.9 squeeze.17
  193.0 0.3 copy.153
  193.3 0.9 squeeze.18
  194.2 0.7 copy.175
  (52 shorter events, 0.6 us)
Async XLA Ops:
  0.6 4.9 %copy-start = (bf16[16,1024]{1,0:T(8,128)(2,1)S(1)}, bf16[16,1024]{1,0:T(8,128)(2,1)}, u32[]{:S(2)}) copy-start(bf16[16,1024]{1,0:T(8,128)(2,1)} %param.13) | copy-start | bytes 98308
  0.6 3.6 %copy-start.4 = (bf16[256,1024]{1,0:T(8,128)(2,1)S(1)}, bf16[256,1024]{1,0:T(8,128)(2,1)}, u32[]{:S(2)}) copy-start(bf16[256,1024]{1,0:T(8,128)(2,1)} %param.12) | copy-start | bytes 1572868
  4.0 1.4 copy-start.7
  4.0 1.5 copy-start.5
  4.3 1.3 copy-start.1
  5.5 3.1 %copy-start.10 = (s32[16,1]{0,1:T(1,128)S(1)}, s32[16,1]{0,1:T(1,128)}, u32[]{:S(2)}) copy-start(s32[16,1]{0,1:T(1,128)} %param.16) | copy-start | bytes 196
  6.6 2.9 %copy-start.2 = (bf16[8,16,1792]{2,1,0:T(8,128)(2,1)}, bf16[8,16,1792]{2,1,0:T(8,128)(2,1)S(1)}, u32[]{:S(2)}) copy-start(bf16[8,16,1792]{2,1,0:T(8,128)(2,1)S(1)} %fusion.18.refs_0_) | copy-start | bytes 1376260
  49.4 35.9 %copy-start.3 = (f32[8,16,128]{2,1,0:T(8,128)S(1)}, f32[8,16,128]{2,1,0:T(8,128)}, u32[]{:S(2)}) copy-start(f32[8,16,128]{2,1,0:T(8,128)} %get-tuple-element.12) | copy-start | bytes 196612
  95.2 1.7 copy-start.6
  135.7 1.0 copy-start.9
  191.7 2.4 %copy-start.8 = (bf16[8,16,512]{2,1,0:T(8,128)(2,1)S(1)}, bf16[8,16,512]{2,1,0:T(8,128)(2,1)}, u32[]{:S(2)}) copy-start(bf16[8,16,512]{2,1,0:T(8,128)(2,1)} %get-tuple-element.16) | copy-start | bytes 393220

commit v2 on v1

--- a/solution.py
+++ b/solution.py
@@ -229,6 +229,205 @@
     )(*arrays)
 
 
+def place(dp, y, z):
+    return {"dp": dp, "y": y, "z": z}
+
+
+def coordinates():
+    return lax.axis_index("dp"), lax.axis_index("y"), lax.axis_index("z")
+
+
+def push(src, dst, send_sem, recv_sem, device):
+    return pltpu.make_async_remote_copy(
+        src_ref=src, dst_ref=dst, send_sem=send_sem, recv_sem=recv_sem,
+        device_id=device, device_id_type=pl.DeviceIdType.MESH,
+    )
+
+
+def others(n, own, body):
+    def step(i, carry):
+        body(lax.rem(own + i, n))
+        return carry
+
+    lax.fori_loop(1, n, step, 0)
+
+
+def greet_rings(sizes):
+    dp, y, z = coordinates()
+    ndp, ny, nz = sizes
+    barrier = pltpu.get_barrier_semaphore()
+
+    def hello(device):
+        pl.semaphore_signal(barrier, inc=1, device_id=device, device_id_type=pl.DeviceIdType.MESH)
+
+    others(nz, z, lambda j: hello(place(dp, y, j)))
+    others(ny, y, lambda j: hello(place(dp, j, z)))
+    others(ndp, dp, lambda j: hello(place(j, y, z)))
+    pl.semaphore_wait(barrier, nz + ny + ndp - 3)
+
+
+def fetch_kernel(sizes, ad, kv, packet, facts, ad_o, kv_o, packet_o, facts_o,
+                 z_send, z_recv, y_send, y_recv, x_send, x_recv, mate_send, mate_recv, own_sem):
+    dp, y, z = coordinates()
+    ndp, ny, nz = sizes
+    nx = ndp // 2
+    x, core = dp // 2, lax.rem(dp, 2)
+    mate = place(2 * x + 1 - core, y, z)
+
+    keep = [
+        pltpu.make_async_copy(ad.at[z], ad_o.at[dp, y, z], own_sem.at[0]),
+        pltpu.make_async_copy(kv.at[z], kv_o.at[y, z], own_sem.at[1]),
+        pltpu.make_async_copy(packet.at[z], packet_o.at[z], own_sem.at[2]),
+        pltpu.make_async_copy(facts.at[z], facts_o.at[z], own_sem.at[3]),
+    ]
+    for copy in keep:
+        copy.start()
+    greet_rings(sizes)
+
+    def z_copy(item, peer, slot):
+        src, dst = [
+            (ad.at[peer], ad_o.at[dp, y, slot]),
+            (kv.at[peer], kv_o.at[y, slot]),
+            (packet.at[peer], packet_o.at[slot]),
+            (facts.at[peer], facts_o.at[slot]),
+        ][item]
+        return push(src, dst, z_send.at[item, peer], z_recv.at[item, slot], place(dp, y, peer))
+
+    def y_copy(item, peer, slot):
+        src, dst = [
+            (ad_o.at[dp, y], ad_o.at[dp, slot]),
+            (kv_o.at[y], kv_o.at[slot]),
+        ][item]
+        return push(src, dst, y_send.at[item, peer], y_recv.at[item, slot], place(dp, peer, z))
+
+    def x_copy(peer, slot):
+        return push(
+            ad_o.at[dp], ad_o.at[2 * slot + core], x_send.at[peer], x_recv.at[slot],
+            place(2 * peer + core, y, z),
+        )
+
+    def mate_copy(block, core_of):
+        slot = 2 * block + core_of
+        return push(ad_o.at[slot], ad_o.at[slot], mate_send.at[block], mate_recv.at[block], mate)
+
+    for item in range(4):
+        others(nz, z, lambda j, item=item: z_copy(item, j, z).start())
+    for item in range(2):
+        others(nz, z, lambda j, item=item: z_copy(item, j, j).wait_recv())
+        keep[item].wait()
+        others(ny, y, lambda j, item=item: y_copy(item, j, y).start())
+    others(ny, y, lambda j: y_copy(0, j, j).wait_recv())
+    others(nx, x, lambda j: x_copy(j, x).start())
+    mate_copy(x, core).start()
+
+    def forward(j):
+        x_copy(j, j).wait_recv()
+        mate_copy(j, core).start()
+
+    others(nx, x, forward)
+    for item in (2, 3):
+        others(nz, z, lambda j, item=item: z_copy(item, j, j).wait_recv())
+        keep[item].wait()
+    others(ny, y, lambda j: y_copy(1, j, j).wait_recv())
+    mate_copy(x, 1 - core).wait_recv()
+    others(nx, x, lambda j: mate_copy(j, 1 - core).wait_recv())
+    for item in range(4):
+        others(nz, z, lambda j, item=item: z_copy(item, j, z).wait_send())
+    for item in range(2):
+        others(ny, y, lambda j, item=item: y_copy(item, j, y).wait_send())
+    others(nx, x, lambda j: x_copy(j, x).wait_send())
+    mate_copy(x, core).wait_send()
+    others(nx, x, lambda j: mate_copy(j, core).wait_send())
+
+
+def fetch(sizes, ad, kv, packet, facts):
+    ndp, ny, nz = sizes
+    shape = jax.ShapeDtypeStruct
+    dma = pltpu.SemaphoreType.DMA
+    vmem = pl.BlockSpec(memory_space=pltpu.VMEM)
+    return pl.pallas_call(
+        functools.partial(fetch_kernel, sizes),
+        out_shape=[
+            shape((ndp, ny) + ad.shape, ad.dtype),
+            shape((ny,) + kv.shape, kv.dtype),
+            shape(packet.shape, packet.dtype),
+            shape(facts.shape, facts.dtype),
+        ],
+        in_specs=[vmem] * 4,
+        out_specs=[vmem] * 4,
+        scratch_shapes=[
+            dma((4, nz)), dma((4, nz)), dma((2, ny)), dma((2, ny)), dma((ndp,)), dma((ndp,)),
+            dma((ndp,)), dma((ndp,)), dma((4,)),
+        ],
+        compiler_params=pltpu.CompilerParams(collective_id=1, has_side_effects=True),
+        name="fetch",
+    )(ad, kv, packet, facts)
+
+
+def settle_kernel(sizes, terms, out, got, total, mid, send, recv, own_sem):
+    dp, y, z = coordinates()
+    ndp, ny, nz = sizes
+    greet_rings(sizes)
+
+    def share_copy(peer, slot):
+        return push(terms.at[peer], got.at[slot], send.at[0, peer], recv.at[0, slot], place(peer, y, z))
+
+    def z_copy(peer, slot):
+        return push(total.at[:, peer], mid.at[slot], send.at[1, peer], recv.at[1, slot], place(dp, y, peer))
+
+    def y_copy(peer, slot):
+        return push(mid.at[:, peer], out.at[dp, slot], send.at[2, peer], recv.at[2, slot], place(dp, peer, z))
+
+    def spread_copy(peer, slot):
+        return push(out.at[dp], out.at[slot], send.at[3, peer], recv.at[3, slot], place(peer, y, z))
+
+    others(ndp, dp, lambda j: share_copy(j, dp).start())
+    acc = terms[dp].astype(jnp.float32)
+    others(ndp, dp, lambda j: share_copy(j, j).wait_recv())
+    for step in range(1, ndp):
+        acc += got[lax.rem(dp + step, ndp)].astype(jnp.float32)
+    total[...] = acc.astype(total.dtype)
+    others(nz, z, lambda j: z_copy(j, z).start())
+    mine = pltpu.make_async_copy(total.at[:, z], mid.at[z], own_sem.at[0])
+    mine.start()
+    others(nz, z, lambda j: z_copy(j, j).wait_recv())
+    mine.wait()
+    others(ny, y, lambda j: y_copy(j, y).start())
+    mine = pltpu.make_async_copy(mid.at[:, y], out.at[dp, y], own_sem.at[1])
+    mine.start()
+    others(ny, y, lambda j: y_copy(j, j).wait_recv())
+    mine.wait()
+    others(ndp, dp, lambda j: spread_copy(j, dp).start())
+    others(ndp, dp, lambda j: spread_copy(j, j).wait_recv())
+    others(ndp, dp, lambda j: share_copy(j, dp).wait_send())
+    others(nz, z, lambda j: z_copy(j, z).wait_send())
+    others(ny, y, lambda j: y_copy(j, y).wait_send())
+    others(ndp, dp, lambda j: spread_copy(j, dp).wait_send())
+
+
+def settle(sizes, terms):
+    ndp, ny, nz = sizes
+    most = max(sizes)
+    block = terms.shape[3:]
+    vmem = pl.BlockSpec(memory_space=pltpu.VMEM)
+    return pl.pallas_call(
+        functools.partial(settle_kernel, sizes),
+        out_shape=jax.ShapeDtypeStruct(terms.shape, terms.dtype),
+        in_specs=[vmem],
+        out_specs=vmem,
+        scratch_shapes=[
+            pltpu.VMEM(terms.shape, terms.dtype),
+            pltpu.VMEM((ny, nz) + block, terms.dtype),
+            pltpu.VMEM((nz, ny) + block, terms.dtype),
+            pltpu.SemaphoreType.DMA((4, most)),
+            pltpu.SemaphoreType.DMA((4, most)),
+            pltpu.SemaphoreType.DMA((2,)),
+        ],
+        compiler_params=pltpu.CompilerParams(collective_id=5, has_side_effects=True),
+        name="settle",
+    )(terms)
+
+
 def compress(keys, values, learned):
     tokens = keys.shape[0]
     k = keys.reshape(tokens, KEY_VALUE_HEADS, HEAD_SIZE)
@@ -269,34 +468,36 @@
     model = queries.shape[1]
     wide = model // nz
     narrow = wide // ny
-    share = RANK // ndp
     rows = nz * SLOTS
     dp, y = lax.axis_index("dp"), lax.axis_index("y")
-    swap = functools.partial(jnp.einsum, "shd->hsd")
 
     live = (jnp.arange(SLOTS, dtype=jnp.int32) < span_len[0, 0])[:, None]
     dy = jnp.where(live, cotangent, jnp.zeros_like(cotangent))
     ck, cv = compress(keys, values, learned)
     out_local, lse = attend_local(queries, keys, values, span_offset[0, 0])
     by_head = lambda array: array.reshape(SLOTS, nz, wide).transpose(1, 0, 2)
-    packet = jnp.concatenate([by_head(queries), by_head(dy), out_local, ck, cv], axis=-1)
+    packet = jnp.concatenate([by_head(queries), by_head(dy), out_local], axis=-1)
     facts = jnp.concatenate([destination.astype(jnp.float32), live.astype(jnp.float32)], axis=1)
     facts = jnp.concatenate([lse, jnp.broadcast_to(facts[None], (nz, SLOTS, 2))], axis=-1)
     facts = jnp.pad(facts, ((0, 0), (0, 0), (0, 128 - facts.shape[-1])))
-    part = lambda adapter: lax.dynamic_slice_in_dim(adapter[0], dp * share, share, 0).reshape(
-        share, nz, wide
-    ).transpose(1, 0, 2)
-    adapters = jnp.concatenate([part(adapter_a), part(adapter_b)], axis=1)
-
-    packet, facts, adapters = exchange(
-        "heads", 1, sizes, (packet, "z_swap"), (facts, "z_swap"), (adapters, "plane")
-    )
+    quarters = wide // 128
+    chunks = jnp.stack([adapter_a[0], adapter_b[0]]).reshape(2, RANK, nz, quarters, 128)
+    chunks = chunks.transpose(0, 3, 2, 1, 4).reshape(2 * quarters, nz, RANK, 128)
+    share = 2 * quarters // ndp
+    ad = lax.dynamic_slice_in_dim(chunks, dp * share, share, 0)
+    ad = ad.transpose(1, 0, 2, 3).reshape(nz, share * RANK, 128)
+
+    ad, short, packet, facts = fetch(
+        sizes, ad, jnp.concatenate([ck, cv], axis=-1), packet, facts
+    )
+    ad = ad.reshape(ndp, decoders, share, RANK, 128)
+    if share > 1:
+        ad = ad.transpose(0, 2, 1, 3, 4)
+    ad = ad.reshape(2, quarters, decoders * RANK, 128)
+    downs, ups = ad[0], ad[1]
     packet = packet.reshape(rows, -1)
     facts = facts.reshape(rows, -1)
     q, dy, out_local = packet[:, :wide], packet[:, wide : 2 * wide], packet[:, 2 * wide : 3 * wide]
-    short, adapters = exchange(
-        "short", 2, sizes, (packet[:, 3 * wide :], "y_spread"), (adapters, "dp_spread")
-    )
     short = short.reshape(ny * rows, 2 * HEAD_SIZE)
     ck, cv = short[:, :HEAD_SIZE], short[:, HEAD_SIZE:]
     lse, target, live = facts[:, :GROUP], facts[:, GROUP : GROUP + 1], facts[:, GROUP + 1 : GROUP + 2]
@@ -320,18 +521,20 @@
     attn = attn.transpose(1, 0, 2).reshape(rows, wide)
     attn = jnp.where(live > 0.5, attn, 0.0).astype(jnp.bfloat16)
 
-    adapters = adapters.reshape(ndp, decoders, 2, share, wide)
-    downs = adapters[:, :, 0].reshape(ndp * decoders * share, wide)
-    ups = adapters[:, :, 1].reshape(ndp * decoders * share, wide)
-    column = jnp.arange(ndp * decoders * share, dtype=jnp.int32)
-    column_decoder = (column // share) % decoders
-    column_rank = column // (share * decoders) * share + column % share
+    column = jnp.arange(decoders * RANK, dtype=jnp.int32)
+    column_decoder, column_rank = column // RANK, column % RANK
     own = target.astype(jnp.int32) == column_decoder[None, :]
     pick = column_rank[:, None] == jnp.arange(RANK, dtype=jnp.int32)[None, :]
     across = (((1,), (1,)), ((), ()))
 
     def narrowed(left, right):
-        full = lax.dot_general(left, right, across, preferred_element_type=jnp.float32)
+        full = sum(
+            lax.dot_general(
+                left[:, 128 * i : 128 * (i + 1)], right[i], across,
+                preferred_element_type=jnp.float32,
+            )
+            for i in range(quarters)
+        )
         return lax.dot_general(
             pick.astype(jnp.float32), jnp.where(own, full, 0.0), (((0,), (1,)), ((), ())),
             precision=HIGH, preferred_element_type=jnp.float32,
@@ -354,7 +557,9 @@
         back, pick.astype(jnp.bfloat16), (((0,), (1,)), ((), ())), preferred_element_type=jnp.float32
     )
     spread = jnp.where(own, spread, 0.0).astype(jnp.bfloat16)
-    dn = jnp.dot(spread, downs, preferred_element_type=jnp.float32)
+    dn = jnp.concatenate(
+        [jnp.dot(spread, downs[i], preferred_element_type=jnp.float32) for i in range(quarters)], axis=1
+    )
     nrm = x * rs_column
     d_rows = (dy.astype(jnp.float32) + rs_column * (dn - nrm * mean_column)).astype(jnp.bfloat16)
     normed = nrm.astype(jnp.bfloat16)
@@ -386,12 +591,10 @@
     from_back = gathered(small[RANK : 2 * RANK])
     is_a = (jnp.arange(2 * narrow, dtype=jnp.int32) < narrow)[None, :]
     terms = jnp.where(is_a, from_back, from_hid).astype(jnp.bfloat16)
-    (terms,) = exchange(
-        "terms", 5, sizes, (terms.reshape(ny, nz * RANK, 2 * narrow), "dp_swap")
-    )
-    terms = jnp.sum(terms.astype(jnp.float32), axis=0).astype(jnp.bfloat16)
-    (grads,) = exchange("owners", 6, sizes, (terms.reshape(nz, RANK, 2 * narrow), "owners"))
-    grads = grads.reshape(ny, nz, RANK, 2, narrow).transpose(3, 2, 1, 0, 4).astype(jnp.float32)
+    terms = terms.reshape(ny, nz, ndp, RANK // ndp, 2 * narrow).transpose(2, 0, 1, 3, 4)
+    grads = settle(sizes, terms)
+    grads = grads.reshape(ndp, ny, nz, RANK // ndp, 2, narrow).transpose(4, 0, 3, 2, 1, 5)
+    grads = grads.astype(jnp.float32)
     grads = grads.reshape(2, 1, RANK, model)
     return grad_rows, grads[0], grads[1]
 

time: 198 us -> 140 us (0.71); the launches traced: 195 us -> 139 us
  Pallas kernels: 148 us -> 99.6 us
  local copies, waits for them, and re-layouts: 21.8 us -> 14.7 us
    pallas_call x6 -> x2, Pallas kernels: 148 us -> 27.1 us  [exchange(): pl.pallas_call(functools.partial(exchange_kernel, kinds, sizes), out_shap...]
    pallas_call x0 -> x2, Pallas kernels: none -> 72.5 us  [the longest x1 46.4 us: fetch(): pl.pallas_call(functools.partial(fetch_kernel, sizes), out_shape=[shape((...]
    slice x3 -> x1, local copies, waits for them, and re-layouts: 3.92 us -> 0.52 us  [narrowed(): right[i]]
    reshape x1 -> x3, local copies, waits for them, and re-layouts: 4.36 us -> 1.1 us  [the longest x1 0.91 us: shards(): terms.reshape(ny, nz, ndp, RANK // ndp, 2 * narrow).transpose(2, 0, 1, 3, 4)]
    dot_general x3 -> x13, matrix products: 3.98 us -> 6.53 us  [the longest x8 4.99 us: narrowed(): lax.dot_general(left[:, 128 * i:128 * (i + 1)], right[i], across, preferr...]
    unnamed x31 -> x34, local copies, waits for them, and re-layouts: 2.86 us -> 4.02 us
where the time goes in v2:
time: 140 us; the launch traced here: 139 us
  Pallas kernels  99.6 us (71%)
  local copies, waits for them, and re-layouts  14.7 us (10%)
  matrix products  12.6 us (9%)
  other arithmetic  9.39 us (7%)
  between operations  2.54 us (2%)
    pallas_call x1, Pallas kernels, fetch(): pl.pallas_call(functools.partial(fetch_kernel, sizes), out_shape=[shape((...  46.4 us
    pallas_call x2, Pallas kernels, exchange(): pl.pallas_call(functools.partial(exchange_kernel, kinds, sizes), out_shap...  27.1 us
    pallas_call x1, Pallas kernels, settle(): pl.pallas_call(functools.partial(settle_kernel, sizes), out_shape=jax.Sha...  26.1 us
    dot_general x8, matrix products, narrowed(): lax.dot_general(left[:, 128 * i:128 * (i + 1)], right[i], across, preferr...  4.99 us
    unnamed x34, local copies, waits for them, and re-layouts  4.02 us

profile of v2, /device:TPU:1, one launch (start us, length us, event | category | flops | bytes accessed | tf_op | source)
XLA Modules:
  0.0 138.9 jit_solution(7368898391181413180)
XLA Ops:
  1.4 1.1 copy.196
  2.6 1.0 reshape.299
  3.6 0.4 fusion.83
  4.0 0.3 fusion.29
  4.4 0.3 fusion.13
  5.5 0.8 pad_maximum_fusion.packet
  6.3 0.1 copy.151
  6.7 0.7 select_maximum_fusion.facts
  7.4 0.2 convolution_multiply_fusion.2
  7.7 0.2 fusion.82
  7.9 0.3 convolution_convert_fusion
  8.2 0.3 convolution_convert_fusion.1
  8.5 0.7 pad_maximum_fusion.3.kv
  9.2 0.2 reshape.292
  9.5 0.6 dynamic-slice_bitcast_fusion.ad
  10.1 46.4 %fetch.1 = (bf16[8,8,8,16,128]{4,3,2,1,0:T(8,128)(2,1)}, bf16[8,8,16,256]{3,2,1,0:T(8,128)(2,1)}, bf16[8,16,1536]{2,1,0:T(8,128)(2,1)}, f32[8,16,128]{2,1,0:T(8,128)}) custom-call(bf16[8,16,128]{2,1,0:T(8,128)(2,1)} %dynamic-slice_bitcast_fusion.ad, bf16[8,16,256]{2,1,0:T(8,128)(2,1)} %pad_maximum_fusion.3.kv, bf16[8,16,1536]{2,1,0:T(8,128)(2,1)} %pad_maximum_fusion.packet, ...), custom_call_target="tpu_custom_call" | custom-call | tf_op jit(solution)/shard_map/fetch/pallas_call | solution.py:348
  56.5 1.1 fusion.81
  57.8 0.1 broadcast_compare_fusion
  57.9 0.3 copy.156
  58.2 1.4 fusion.1
  59.7 0.6 fusion.2
  60.6 0.7 multiply_reduce_fusion
  61.3 0.9 copy-done.1
  62.2 0.5 fusion.79
  62.7 0.2 fusion.59
  63.0 0.3 convolution_add_fusion.5
  63.2 0.2 convolution_add_fusion.4
  63.6 0.3 fusion.5
  63.9 0.6 fusion.33
  64.5 1.0 fusion.54
  65.5 1.0 convolution_add_fusion.2
  66.5 1.0 convolution_add_fusion.1
  67.5 1.0 fusion.4
  68.5 0.6 fusion.31
  69.2 0.7 maximum_maximum_fusion.refs_0_
  69.9 10.9 %sums.1 = f32[8,40,128]{2,1,0:T(8,128)} custom-call(f32[40,128]{1,0:T(8,128)} %maximum_maximum_fusion.refs_0_), custom_call_target="tpu_custom_call" | custom-call | tf_op jit(solution)/shard_map/sums/pallas_call | solution.py:219
  80.8 0.9 reduce_sum.61
  81.7 0.6 pad_maximum_fusion.4.refs_2_
  82.4 0.2 copy.164
  82.5 0.2 fusion.36
  82.9 0.2 copy.165
  83.1 0.9 pad_maximum_fusion.2.refs_1_
  83.9 0.4 fusion.7
  84.4 0.3 fusion.84
  84.6 0.3 fusion.85
  84.9 0.3 fusion.86
  85.2 0.3 fusion.87
  85.6 0.8 copy.163
  86.4 16.2 %rows.1 = (bf16[8,16,512]{2,1,0:T(8,128)(2,1)}, bf16[8,128,128]{2,1,0:T(8,128)(2,1)}, bf16[8,48,128]{2,1,0:T(8,128)(2,1)}) custom-call(bf16[8,16,512]{2,1,0:T(8,128)(2,1)} %bitcast.212, bf16[8,128,128]{2,1,0:T(8,128)(2,1)} %pad_maximum_fusion.2.refs_1_, bf16[48,128]{1,0:T(8,128)(2,1)} %pad_maximum_fusion.4.refs_2_), custom_call_target="tpu_custom_call" | custom-call | tf_op jit(solution)/shard_map/rows/pallas_call | solution.py:219
  102.6 0.8 slice_bitcast_fusion.5
  103.4 0.7 slice_convert_fusion.1
  104.2 0.4 broadcast_select_fusion.1
  104.6 0.6 copy-done.11
  105.1 0.7 convolution_multiply_fusion
  105.9 0.7 fusion.8
  106.6 0.9 copy.232
  107.5 26.1 %settle.1 = bf16[8,8,8,2,128]{4,3,2,1,0:T(2,128)(2,1)} custom-call(bf16[8,8,8,2,128]{4,3,2,1,0:T(2,128)(2,1)} %bitcast.202), custom_call_target="tpu_custom_call" | custom-call | tf_op jit(solution)/shard_map/settle/pallas_call | solution.py:413
  133.6 1.5 %reshape.314 = f32[8,8,8,2,2,64]{5,4,3,2,1,0:T(2,128)S(1)} reshape(bf16[8,8,8,2,128]{4,3,2,1,0:T(2,128)(2,1)} %settle.1) | data formatting | bytes 786432 | tf_op jit(solution)/shard_map/convert_element_type | solution.py:597
  135.2 0.9 fusion.80
  136.1 0.2 copy.170
  136.3 0.9 squeeze.53
  137.2 0.2 copy.171
  137.3 0.9 squeeze.54
  138.2 0.7 copy.193
  (66 shorter events, 1.9 us)
Async XLA Ops:
  0.6 6.8 %copy-start = (bf16[16,1024]{1,0:T(8,128)(2,1)S(1)}, bf16[16,1024]{1,0:T(8,128)(2,1)}, u32[]{:S(2)}) copy-start(bf16[16,1024]{1,0:T(8,128)(2,1)} %param.13) | copy-start | bytes 98308
  0.6 3.6 %copy-start.4 = (bf16[256,1024]{1,0:T(8,128)(2,1)S(1)}, bf16[256,1024]{1,0:T(8,128)(2,1)}, u32[]{:S(2)}) copy-start(bf16[256,1024]{1,0:T(8,128)(2,1)} %param.12) | copy-start | bytes 1572868
  4.0 1.4 %copy-start.7 = (bf16[16,4096]{1,0:T(8,128)(2,1)S(1)}, bf16[16,4096]{1,0:T(8,128)(2,1)}, u32[]{:S(2)}) copy-start(bf16[16,4096]{1,0:T(8,128)(2,1)} %param.17) | copy-start | bytes 393220
  4.3 1.2 copy-start.5
  4.4 2.2 %copy-start.12 = (s32[16,1]{0,1:T(1,128)S(1)}, s32[16,1]{0,1:T(1,128)}, u32[]{:S(2)}) copy-start(s32[16,1]{0,1:T(1,128)} %param.16) | copy-start | bytes 196
  4.4 3.0 %copy-start.2 = (bf16[256,1024]{1,0:T(8,128)(2,1)S(1)}, bf16[256,1024]{1,0:T(8,128)(2,1)}, u32[]{:S(2)}) copy-start(bf16[256,1024]{1,0:T(8,128)(2,1)} %param.11) | copy-start | bytes 1572868
  6.3 2.8 %copy-start.9 = (bf16[1,16,4096]{2,1,0:T(8,128)(2,1)S(1)}, bf16[1,16,4096]{2,1,0:T(8,128)(2,1)}, u32[]{:S(2)}) copy-start(bf16[1,16,4096]{2,1,0:T(8,128)(2,1)} %param.19) | copy-start | bytes 393220
  6.3 2.8 %copy-start.10 = (bf16[1,16,4096]{2,1,0:T(8,128)(2,1)S(1)}, bf16[1,16,4096]{2,1,0:T(8,128)(2,1)}, u32[]{:S(2)}) copy-start(bf16[1,16,4096]{2,1,0:T(8,128)(2,1)} %param.18) | copy-start | bytes 393220
  56.5 3.1 %copy-start.3 = (f32[8,16,128]{2,1,0:T(8,128)S(1)}, f32[8,16,128]{2,1,0:T(8,128)}, u32[]{:S(2)}) copy-start(f32[8,16,128]{2,1,0:T(8,128)} %get-tuple-element.11) | copy-start | bytes 196612
  59.6 1.0 copy-start.6
  60.6 1.6 %copy-start.1 = (bf16[8,8,8,16,128]{4,3,2,1,0:T(8,128)(2,1)S(1)}, bf16[8,8,8,16,128]{4,3,2,1,0:T(8,128)(2,1)}, u32[]{:S(2)}) copy-start(bf16[8,8,8,16,128]{4,3,2,1,0:T(8,128)(2,1)} %get-tuple-element.13) | copy-start | bytes 6291460
  104.2 1.0 copy-start.11
  136.1 2.1 %copy-start.8 = (bf16[8,16,512]{2,1,0:T(8,128)(2,1)S(1)}, bf16[8,16,512]{2,1,0:T(8,128)(2,1)}, u32[]{:S(2)}) copy-start(bf16[8,16,512]{2,1,0:T(8,128)(2,1)} %get-tuple-element.14) | copy-start | bytes 393220

commit v3 on v2

--- a/solution.py
+++ b/solution.py
@@ -493,7 +493,8 @@
     ad = ad.reshape(ndp, decoders, share, RANK, 128)
     if share > 1:
         ad = ad.transpose(0, 2, 1, 3, 4)
-    ad = ad.reshape(2, quarters, decoders * RANK, 128)
+    ad = ad.reshape(2, quarters, decoders * RANK, 128).transpose(0, 2, 1, 3)
+    ad = ad.reshape(2, decoders * RANK, wide)
     downs, ups = ad[0], ad[1]
     packet = packet.reshape(rows, -1)
     facts = facts.reshape(rows, -1)
@@ -528,13 +529,7 @@
     across = (((1,), (1,)), ((), ()))
 
     def narrowed(left, right):
-        full = sum(
-            lax.dot_general(
-                left[:, 128 * i : 128 * (i + 1)], right[i], across,
-                preferred_element_type=jnp.float32,
-            )
-            for i in range(quarters)
-        )
+        full = lax.dot_general(left, right, across, preferred_element_type=jnp.float32)
         return lax.dot_general(
             pick.astype(jnp.float32), jnp.where(own, full, 0.0), (((0,), (1,)), ((), ())),
             precision=HIGH, preferred_element_type=jnp.float32,
@@ -545,7 +540,9 @@
     partial = jnp.concatenate(
         [narrowed(attn, downs), narrowed(dy, ups), square, jnp.zeros((7, rows), jnp.float32)], axis=0
     )
-    (partial,) = exchange("sums", 3, sizes, (partial, "z_spread"))
+    slices = lambda array: array.reshape(rows, ny, narrow).transpose(1, 0, 2)
+    columns = jnp.concatenate([slices(attn), slices(dy)], axis=-1)
+    partial, columns = exchange("sums", 3, sizes, (partial, "z_spread"), (columns, "y_swap"))
     sums = jnp.sum(partial, axis=0)
     rs = lax.rsqrt(sums[2 * RANK : 2 * RANK + 1] / model + EPS)
     hid_exact = sums[:RANK] * rs
@@ -557,21 +554,16 @@
         back, pick.astype(jnp.bfloat16), (((0,), (1,)), ((), ())), preferred_element_type=jnp.float32
     )
     spread = jnp.where(own, spread, 0.0).astype(jnp.bfloat16)
-    dn = jnp.concatenate(
-        [jnp.dot(spread, downs[i], preferred_element_type=jnp.float32) for i in range(quarters)], axis=1
-    )
+    dn = jnp.dot(spread, downs, preferred_element_type=jnp.float32)
     nrm = x * rs_column
     d_rows = (dy.astype(jnp.float32) + rs_column * (dn - nrm * mean_column)).astype(jnp.bfloat16)
-    normed = nrm.astype(jnp.bfloat16)
-
-    slices = lambda array: array.reshape(rows, ny, narrow).transpose(1, 0, 2)
-    columns = jnp.concatenate([slices(normed), slices(dy)], axis=-1)
+
+    scaled = (back.astype(jnp.float32) * rs).astype(jnp.bfloat16)
     small = jnp.concatenate(
-        [hid, back, jnp.broadcast_to(target.T, (RANK, rows)).astype(jnp.bfloat16)], axis=0
-    )
-    d_rows, columns, small = exchange(
-        "rows", 4, sizes,
-        (d_rows.reshape(nz, SLOTS, wide), "z_swap"), (columns, "y_swap"), (small, "y_spread"),
+        [hid, scaled, jnp.broadcast_to(target.T, (RANK, rows)).astype(jnp.bfloat16)], axis=0
+    )
+    d_rows, small = exchange(
+        "rows", 4, sizes, (d_rows.reshape(nz, SLOTS, wide), "z_swap"), (small, "y_spread")
     )
     grad_rows = d_rows.transpose(1, 0, 2).reshape(SLOTS, model)
     columns = columns.reshape(ny * rows, 2 * narrow)
@@ -593,10 +585,8 @@
     terms = jnp.where(is_a, from_back, from_hid).astype(jnp.bfloat16)
     terms = terms.reshape(ny, nz, ndp, RANK // ndp, 2 * narrow).transpose(2, 0, 1, 3, 4)
     grads = settle(sizes, terms)
-    grads = grads.reshape(ndp, ny, nz, RANK // ndp, 2, narrow).transpose(4, 0, 3, 2, 1, 5)
-    grads = grads.astype(jnp.float32)
-    grads = grads.reshape(2, 1, RANK, model)
-    return grad_rows, grads[0], grads[1]
+    final = lambda part: part.transpose(0, 3, 2, 1, 4).reshape(1, RANK, model).astype(jnp.float32)
+    return grad_rows, final(grads[..., :narrow]), final(grads[..., narrow:])
 
 
 def solution(mesh):

time: 140 us -> 143 us (1.021)
  other arithmetic: 9.39 us -> 12.5 us
  Pallas kernels: 99.6 us -> 97.7 us
  local copies, waits for them, and re-layouts: 14.7 us -> 16.5 us
    another operation x0 -> x1, local copies, waits for them, and re-layouts: none -> 3 us  [shards(): ad = ad.reshape(2, quarters, decoders * RANK, 128).transpose(0, 2, 1, 3)]
    pallas_call x2, Pallas kernels: 27.1 us -> 24.4 us  [exchange(): pl.pallas_call(functools.partial(exchange_kernel, kinds, sizes), out_shap...]
    unnamed x34 -> x26, local copies, waits for them, and re-layouts: 4.02 us -> 1.78 us
    dot_general x13 -> x3, matrix products: 6.53 us -> 4.29 us  [the longest x1 2.32 us: shards(): dn = jnp.dot(spread, downs, preferred_element_type=jnp.float32)]
    squeeze x2 -> x0, local copies, waits for them, and re-layouts: 1.77 us -> none  [shards(): return (grad_rows, grads[0], grads[1])]
    dot_general x1, matrix products: 0.67 us -> 2.37 us  [shards(): jnp.einsum('grk,kd->grd', prob.astype(jnp.bfloat16), cv, preferred_elemen...]
    convert_element_type x1, local copies, waits for them, and re-layouts: 0.12 us -> 1.79 us  [shards(): out_local.reshape(rows, GROUP, HEAD_SIZE).transpose(1, 0, 2)]
where the time goes in v3:
time: 143 us; the launch traced here: 142 us
  Pallas kernels  97.7 us (68%)
  local copies, waits for them, and re-layouts  16.5 us (12%)
  matrix products  13.2 us (9%)
  other arithmetic  12.5 us (9%)
  between operations  2.36 us (2%)
    pallas_call x1, Pallas kernels, fetch(): pl.pallas_call(functools.partial(fetch_kernel, sizes), out_shape=[shape((...  46.5 us
    pallas_call x1, Pallas kernels, settle(): pl.pallas_call(functools.partial(settle_kernel, sizes), out_shape=jax.Sha...  26.8 us
    pallas_call x2, Pallas kernels, exchange(): pl.pallas_call(functools.partial(exchange_kernel, kinds, sizes), out_shap...  24.4 us
    another operation x1, local copies, waits for them, and re-layouts, shards(): ad = ad.reshape(2, quarters, decoders * RANK, 128).transpose(0, 2, 1, 3)  3 us

profile of v3, /device:TPU:1, one launch (start us, length us, event | category | flops | bytes accessed | tf_op | source)
XLA Modules:
  0.0 142.2 jit_solution(7340367662947286628)
XLA Ops:
  0.7 1.1 pad_maximum_fusion.1
  1.8 0.2 reshape.300
  1.9 0.1 copy.136
  2.0 0.6 dynamic-slice_bitcast_fusion.ad
  2.7 1.3 convolution_multiply_fusion.2
  3.9 0.2 fusion.80
  4.2 0.3 convolution_convert_fusion
  4.5 0.3 convolution_convert_fusion.1
  4.8 0.7 pad_maximum_fusion.3.kv
  5.4 0.1 copy.194
  5.5 0.1 copy.193
  6.5 0.4 fusion.81
  6.9 0.3 fusion.33
  7.2 0.3 fusion.16
  8.2 0.1 broadcast_select_fusion.2
  8.3 0.8 pad_maximum_fusion.packet
  9.1 0.1 copy.150
  9.2 0.1 copy.148
  9.3 0.1 copy.149
  9.5 0.7 select_maximum_fusion.facts
  10.2 46.5 %fetch.1 = (bf16[8,8,8,16,128]{4,3,2,1,0:T(8,128)(2,1)}, bf16[8,8,16,256]{3,2,1,0:T(8,128)(2,1)}, bf16[8,16,1536]{2,1,0:T(8,128)(2,1)}, f32[8,16,128]{2,1,0:T(8,128)}) custom-call(bf16[8,16,128]{2,1,0:T(8,128)(2,1)} %dynamic-slice_bitcast_fusion.ad, bf16[8,16,256]{2,1,0:T(8,128)(2,1)} %pad_maximum_fusion.3.kv, bf16[8,16,1536]{2,1,0:T(8,128)(2,1)} %pad_maximum_fusion.packet, ...), custom_call_target="tpu_custom_call" | custom-call | tf_op jit(solution)/shard_map/fetch/pallas_call | solution.py:348
  56.7 3.0 %copy.160 = bf16[2,4,1024,128]{2,3,1,0:T(8,128)(2,1)S(1)} copy(bf16[2,4,1024,128]{3,2,1,0:T(8,128)(2,1)} %bitcast.169) | data formatting | bytes 4194304 | tf_op jit(solution)/shard_map/reshape;reshape | solution.py:496
  59.7 1.2 fusion.78
  60.9 0.1 slice.78
  61.1 0.1 slice_compare_fusion
  61.3 0.2 broadcast_compare_fusion
  61.4 0.3 copy.153
  61.7 1.8 %fusion.79 = (bf16[128,512]{1,0:T(8,128)(2,1)S(1)}, f32[128,512]{1,0:T(8,128)}, bf16[128,512]{1,0:T(8,128)(2,1)S(1)}) fusion(bf16[128,1536]{1,0:T(8,128)(2,1)} %bitcast.175), kind=kLoop, calls=%fused_computation.147 | loop fusion | flops 65536 | bytes 917504 | tf_op jit(solution)/shard_map/slice | solution.py:501
  63.5 0.8 copy.154
  64.2 1.4 fusion.1
  65.7 0.5 fusion.2
  66.3 1.8 %copy.159 = f32[128,512]{0,1:T(8,128)} copy(f32[128,512]{1,0:T(8,128)} %get-tuple-element.26) | data formatting | bytes 524288 | tf_op jit(solution)/shard_map/convert_element_type | solution.py:520
  68.1 2.4 %multiply_reduce_fusion = (f32[128]{0:T(128)S(1)}, bf16[128,4,128]{0,2,1:T(8,128)(2,1)}, bf16[128,4,128]{0,2,1:T(8,128)(2,1)}) fusion(pred[128]{0:T(512)(128)(4,1)S(1)} %bitcast.205, f32[128,4]{0,1:T(4,128)S(1)} %get-tuple-element.21, f32[128,4,128]{0,2,1:T(8,128)} %bitcast.192, f32[128,4]{0,1:T(4,128)S(1)} %get-tuple-element.22, ...), kind=kOutput, calls=%fused_computation.66 | convolution fusion | flops 137363328 | bytes 3021440 | tf_op jit(solution)/shard_map/grk,kd->grd/dot_general | solution.py:517
  70.4 1.0 copy.164
  71.5 1.6 %convolution_select_fusion.2 = f32[128,1024]{1,0:T(8,128)S(1)} fusion(bf16[1024,512]{0,1:T(8,128)(2,1)} %bitcast.167, s32[1024]{0:T(1024)S(1)} %get-tuple-element.46, s32[128]{0:T(128)S(1)} %get-tuple-element.38, bf16[128,1536]{1,0:T(8,128)(2,1)} %bitcast.176), kind=kOutput, calls=%fused_computation.10 | convolution fusion | flops 134479872 | bytes 1708544 | tf_op jit(solution)/shard_map/dot_general | solution.py:532
  73.1 0.6 fusion.35
  73.7 0.4 convolution_select_fusion.3
  74.1 0.6 fusion.37
  74.6 0.1 pad.13.clone
  74.8 0.7 maximum_maximum_fusion.refs_0_
  75.4 0.1 copy.162
  75.6 0.2 copy.163
  75.8 0.2 copy.161
  76.0 0.1 fusion.40
  76.1 0.9 pad_maximum_fusion.2.refs_1_
  76.9 13.3 %sums.1 = (f32[8,40,128]{2,1,0:T(8,128)}, bf16[8,128,128]{2,1,0:T(8,128)(2,1)}) custom-call(f32[40,128]{1,0:T(8,128)} %maximum_maximum_fusion.refs_0_, bf16[8,128,128]{2,1,0:T(8,128)(2,1)} %pad_maximum_fusion.2.refs_1_), custom_call_target="tpu_custom_call" | custom-call | tf_op jit(solution)/shard_map/sums/pallas_call | solution.py:219
  90.3 0.9 reduce_sum.61
  91.3 2.3 %fusion.13 = bf16[128,512]{1,0:T(8,128)(2,1)} fusion(bf16[1024,512]{0,1:T(8,128)(2,1)S(1)} %bitcast.166, s32[1024]{0:T(1024)S(1)} %get-tuple-element.46, s32[1024]{0:T(1024)S(1)} %get-tuple-element.47, s32[128]{0:T(128)S(1)} %get-tuple-element.38, bf16[128,512]{1,0:T(8,128)(2,1)S(1)} %copy.164, f32[128]{0:T(128)S(1)} %broadcast_multiply_fusion, ...), kind=kOutput, calls=%fused_computation.25 | convolution fusion | flops 139415552 | bytes 1460224 | tf_op jit(solution)/shard_map/dot_general | solution.py:557
  93.6 0.6 pad_maximum_fusion.4.refs_1_
  94.2 11.1 %rows.1 = (bf16[8,16,512]{2,1,0:T(8,128)(2,1)}, bf16[8,48,128]{2,1,0:T(8,128)(2,1)}) custom-call(bf16[8,16,512]{2,1,0:T(8,128)(2,1)} %bitcast.200, bf16[48,128]{1,0:T(8,128)(2,1)} %pad_maximum_fusion.4.refs_1_), custom_call_target="tpu_custom_call" | custom-call | tf_op jit(solution)/shard_map/rows/pallas_call | solution.py:219
  105.3 1.6 %copy.190 = bf16[8,2,8,512]{3,2,0,1:T(8,128)(2,1)} copy(bf16[8,2,8,512]{3,2,1,0:T(8,128)(2,1)} %bitcast.201) | data formatting | bytes 262144 | tf_op jit(solution)/shard_map/reshape | solution.py:568
  106.8 0.7 slice_convert_fusion.1
  107.6 0.8 slice_bitcast_fusion.5
  108.4 0.4 broadcast_select_fusion.1
  108.8 0.6 copy-done.8
  109.4 0.7 convolution_multiply_fusion
  110.1 0.7 fusion.6
  110.8 0.9 copy.229
  111.7 26.8 %settle.1 = bf16[8,8,8,2,128]{4,3,2,1,0:T(2,128)(2,1)} custom-call(bf16[8,8,8,2,128]{4,3,2,1,0:T(2,128)(2,1)} %bitcast.174), custom_call_target="tpu_custom_call" | custom-call | tf_op jit(solution)/shard_map/settle/pallas_call | solution.py:413
  138.5 1.5 %convert_bitcast_fusion = (f32[8,2,8,8,64]{4,1,2,3,0:T(2,128)S(1)}, f32[8,2,8,8,64]{4,1,2,3,0:T(2,128)S(1)}) fusion(bf16[8,8,8,2,128]{4,3,2,1,0:T(2,128)(2,1)} %settle.1), kind=kLoop, calls=%fused_computation.44 | loop fusion | flops 131072 | bytes 786432 | tf_op jit(solution)/shard_map/convert_element_type | solution.py:588
  140.0 0.2 copy.169
  140.2 0.9 reshape.322
  141.1 0.2 copy.170
  141.3 0.9 reshape.323
  (48 shorter events, 0.6 us)
Async XLA Ops:
  0.6 2.0 %copy-start = (bf16[16,1024]{1,0:T(8,128)(2,1)S(1)}, bf16[16,1024]{1,0:T(8,128)(2,1)}, u32[]{:S(2)}) copy-start(bf16[16,1024]{1,0:T(8,128)(2,1)} %param.13) | copy-start | bytes 98308
  0.6 3.8 %copy-start.1 = (bf16[256,1024]{1,0:T(8,128)(2,1)S(1)}, bf16[256,1024]{1,0:T(8,128)(2,1)}, u32[]{:S(2)}) copy-start(bf16[256,1024]{1,0:T(8,128)(2,1)} %param.11) | copy-start | bytes 1572868
  0.7 3.5 %copy-start.4 = (bf16[256,1024]{1,0:T(8,128)(2,1)S(1)}, bf16[256,1024]{1,0:T(8,128)(2,1)}, u32[]{:S(2)}) copy-start(bf16[256,1024]{1,0:T(8,128)(2,1)} %param.12) | copy-start | bytes 1572868
  4.2 1.5 %copy-start.5 = (bf16[16,4096]{1,0:T(8,128)(2,1)S(1)}, bf16[16,4096]{1,0:T(8,128)(2,1)}, u32[]{:S(2)}) copy-start(bf16[16,4096]{1,0:T(8,128)(2,1)} %param.10) | copy-start | bytes 393220
  6.5 1.7 %copy-start.7 = (bf16[16,4096]{1,0:T(8,128)(2,1)S(1)}, bf16[16,4096]{1,0:T(8,128)(2,1)}, u32[]{:S(2)}) copy-start(bf16[16,4096]{1,0:T(8,128)(2,1)} %param.17) | copy-start | bytes 393220
  7.1 1.9 %copy-start.9 = (s32[16,1]{0,1:T(1,128)S(1)}, s32[16,1]{0,1:T(1,128)}, u32[]{:S(2)}) copy-start(s32[16,1]{0,1:T(1,128)} %param.16) | copy-start | bytes 196
  59.7 1.3 copy-start.2
  70.4 3.3 %copy-start.6 = (bf16[128,4,128]{0,2,1:T(8,128)(2,1)S(1)}, bf16[128,4,128]{0,2,1:T(8,128)(2,1)}, u32[]{:S(2)}) copy-start(bf16[128,4,128]{0,2,1:T(8,128)(2,1)} %get-tuple-element.20) | copy-start | bytes 393220
  73.1 2.7 %copy-start.3 = (bf16[128,4,128]{0,2,1:T(8,128)(2,1)S(1)}, bf16[128,4,128]{0,2,1:T(8,128)(2,1)}, u32[]{:S(2)}) copy-start(bf16[128,4,128]{0,2,1:T(8,128)(2,1)} %get-tuple-element.43) | copy-start | bytes 393220
  108.4 1.0 copy-start.8

commit v4 on v3

--- a/solution.py
+++ b/solution.py
@@ -493,8 +493,7 @@
     ad = ad.reshape(ndp, decoders, share, RANK, 128)
     if share > 1:
         ad = ad.transpose(0, 2, 1, 3, 4)
-    ad = ad.reshape(2, quarters, decoders * RANK, 128).transpose(0, 2, 1, 3)
-    ad = ad.reshape(2, decoders * RANK, wide)
+    ad = ad.reshape(2, quarters, decoders * RANK, 128)
     downs, ups = ad[0], ad[1]
     packet = packet.reshape(rows, -1)
     facts = facts.reshape(rows, -1)
@@ -529,7 +528,13 @@
     across = (((1,), (1,)), ((), ()))
 
     def narrowed(left, right):
-        full = lax.dot_general(left, right, across, preferred_element_type=jnp.float32)
+        full = sum(
+            lax.dot_general(
+                left[:, 128 * i : 128 * (i + 1)], right[i], across,
+                preferred_element_type=jnp.float32,
+            )
+            for i in range(quarters)
+        )
         return lax.dot_general(
             pick.astype(jnp.float32), jnp.where(own, full, 0.0), (((0,), (1,)), ((), ())),
             precision=HIGH, preferred_element_type=jnp.float32,
@@ -554,7 +559,9 @@
         back, pick.astype(jnp.bfloat16), (((0,), (1,)), ((), ())), preferred_element_type=jnp.float32
     )
     spread = jnp.where(own, spread, 0.0).astype(jnp.bfloat16)
-    dn = jnp.dot(spread, downs, preferred_element_type=jnp.float32)
+    dn = jnp.concatenate(
+        [jnp.dot(spread, downs[i], preferred_element_type=jnp.float32) for i in range(quarters)], axis=1
+    )
     nrm = x * rs_column
     d_rows = (dy.astype(jnp.float32) + rs_column * (dn - nrm * mean_column)).astype(jnp.bfloat16)
 

time: 143 us -> 140 us (0.979)
  local copies, waits for them, and re-layouts: 16.5 us -> 12 us
    another operation x1 -> x0, local copies, waits for them, and re-layouts: 3 us -> none  [shards(): ad = ad.reshape(2, quarters, decoders * RANK, 128).transpose(0, 2, 1, 3)]
    dot_general x3 -> x13, matrix products: 4.29 us -> 6.45 us  [the longest x8 4.92 us: narrowed(): lax.dot_general(left[:, 128 * i:128 * (i + 1)], right[i], across, preferr...]
    dot_general x1, matrix products: 2.37 us -> 0.67 us  [shards(): jnp.einsum('grk,kd->grd', prob.astype(jnp.bfloat16), cv, preferred_elemen...]
    convert_element_type x1, local copies, waits for them, and re-layouts: 1.79 us -> 0.12 us  [shards(): out_local.reshape(rows, GROUP, HEAD_SIZE).transpose(1, 0, 2)]
    slice x3 -> x1, local copies, waits for them, and re-layouts: 2.12 us -> 0.52 us  [narrowed(): right[i]]
    unnamed x26 -> x28, local copies, waits for them, and re-layouts: 1.78 us -> 2.93 us
where the time goes in v4:
time: 140 us; the launch traced here: 138 us
  Pallas kernels  97.7 us (70%)
  matrix products  13.7 us (10%)
  other arithmetic  12.7 us (9%)
  local copies, waits for them, and re-layouts  12 us (9%)
  between operations  2.45 us (2%)
    pallas_call x1, Pallas kernels, fetch(): pl.pallas_call(functools.partial(fetch_kernel, sizes), out_shape=[shape((...  46.4 us
    pallas_call x1, Pallas kernels, settle(): pl.pallas_call(functools.partial(settle_kernel, sizes), out_shape=jax.Sha...  27.1 us
    pallas_call x2, Pallas kernels, exchange(): pl.pallas_call(functools.partial(exchange_kernel, kinds, sizes), out_shap...  24.2 us
    dot_general x8, matrix products, narrowed(): lax.dot_general(left[:, 128 * i:128 * (i + 1)], right[i], across, preferr...  4.92 us
    unnamed x28, local copies, waits for them, and re-layouts  2.93 us

profile of v4, /device:TPU:1, one launch (start us, length us, event | category | flops | bytes accessed | tf_op | source)
XLA Modules:
  0.0 138.5 jit_solution(16303957723072025500)
XLA Ops:
  0.7 1.1 pad_maximum_fusion.1
  1.8 0.2 reshape.309
  2.1 0.6 dynamic-slice_bitcast_fusion.ad
  2.7 1.3 convolution_multiply_fusion.2
  3.9 0.2 fusion.83
  4.2 0.3 convolution_convert_fusion
  4.5 0.3 convolution_convert_fusion.1
  4.8 0.7 pad_maximum_fusion.3.kv
  6.5 0.4 fusion.84
  6.9 0.3 fusion.29
  7.2 0.3 fusion.13
  8.3 0.8 pad_maximum_fusion.packet
  9.2 0.1 copy.148
  9.3 0.1 copy.149
  9.4 0.7 select_maximum_fusion.facts
  10.2 46.4 %fetch.1 = (bf16[8,8,8,16,128]{4,3,2,1,0:T(8,128)(2,1)}, bf16[8,8,16,256]{3,2,1,0:T(8,128)(2,1)}, bf16[8,16,1536]{2,1,0:T(8,128)(2,1)}, f32[8,16,128]{2,1,0:T(8,128)}) custom-call(bf16[8,16,128]{2,1,0:T(8,128)(2,1)} %dynamic-slice_bitcast_fusion.ad, bf16[8,16,256]{2,1,0:T(8,128)(2,1)} %pad_maximum_fusion.3.kv, bf16[8,16,1536]{2,1,0:T(8,128)(2,1)} %pad_maximum_fusion.packet, ...), custom_call_target="tpu_custom_call" | custom-call | tf_op jit(solution)/shard_map/fetch/pallas_call | solution.py:348
  56.6 0.9 slice.160
  57.6 1.0 slice_compare_fusion
  58.6 0.1 broadcast_compare_fusion
  58.8 0.3 copy.154
  59.0 1.1 fusion.82
  60.3 1.4 %fusion.1 = (f32[4,128]{1,0:T(4,128)S(1)}, f32[1024,128,4]{1,0,2:T(8,128)S(1)}) fusion(pred[128,1024]{0,1:T(8,128)(4,1)S(1)} %copy.154, bf16[128,4,128]{0,2,1:T(8,128)(2,1)S(1)} %bitcast.212, bf16[1024,256]{1,0:T(8,128)(2,1)} %bitcast.225), kind=kOutput, calls=%fused_computation.5 | convolution fusion | flops 135790080 | bytes 2623488 | tf_op jit(solution)/shard_map/rgd,kd->grk/dot_general | solution.py:506
  61.8 0.5 fusion.2
  62.5 0.7 multiply_reduce_fusion
  63.2 0.9 copy-done.1
  64.1 0.5 fusion.81
  64.6 1.0 fusion.54
  65.6 1.0 convolution_add_fusion.2
  66.6 1.0 convolution_add_fusion.1
  67.6 1.0 fusion.4
  68.6 0.6 fusion.31
  69.2 0.2 fusion.59
  69.5 0.3 convolution_add_fusion.5
  69.7 0.2 convolution_add_fusion.4
  70.0 0.2 fusion.5
  70.2 0.6 fusion.33
  70.9 0.7 maximum_maximum_fusion.refs_0_
  71.7 0.2 copy.162
  71.9 0.2 copy.161
  72.2 0.9 pad_maximum_fusion.2.refs_1_
  73.1 13.3 %sums.1 = (f32[8,40,128]{2,1,0:T(8,128)}, bf16[8,128,128]{2,1,0:T(8,128)(2,1)}) custom-call(f32[40,128]{1,0:T(8,128)} %maximum_maximum_fusion.refs_0_, bf16[8,128,128]{2,1,0:T(8,128)(2,1)} %pad_maximum_fusion.2.refs_1_), custom_call_target="tpu_custom_call" | custom-call | tf_op jit(solution)/shard_map/sums/pallas_call | solution.py:219
  86.4 0.9 reduce_sum.61
  87.4 0.4 fusion.7
  87.8 0.3 fusion.88
  88.1 0.3 fusion.87
  88.4 0.3 fusion.86
  88.6 0.3 fusion.85
  89.1 0.8 copy.163
  89.8 0.6 pad_maximum_fusion.4.refs_1_
  90.4 10.8 %rows.1 = (bf16[8,16,512]{2,1,0:T(8,128)(2,1)}, bf16[8,48,128]{2,1,0:T(8,128)(2,1)}) custom-call(bf16[8,16,512]{2,1,0:T(8,128)(2,1)} %bitcast.216, bf16[48,128]{1,0:T(8,128)(2,1)} %pad_maximum_fusion.4.refs_1_), custom_call_target="tpu_custom_call" | custom-call | tf_op jit(solution)/shard_map/rows/pallas_call | solution.py:219
  101.3 1.6 %copy.191 = bf16[8,2,8,512]{3,2,0,1:T(8,128)(2,1)} copy(bf16[8,2,8,512]{3,2,1,0:T(8,128)(2,1)} %bitcast.228) | data formatting | bytes 262144 | tf_op jit(solution)/shard_map/reshape | solution.py:575
  102.9 0.7 slice_convert_fusion.1
  103.6 0.8 slice_bitcast_fusion.5
  104.5 0.4 broadcast_select_fusion.1
  104.8 0.6 copy-done.8
  105.4 0.7 convolution_multiply_fusion
  106.1 0.7 fusion.8
  106.8 0.9 copy.230
  107.7 27.1 %settle.1 = bf16[8,8,8,2,128]{4,3,2,1,0:T(2,128)(2,1)} custom-call(bf16[8,8,8,2,128]{4,3,2,1,0:T(2,128)(2,1)} %bitcast.203), custom_call_target="tpu_custom_call" | custom-call | tf_op jit(solution)/shard_map/settle/pallas_call | solution.py:413
  134.9 1.5 %convert_bitcast_fusion = (f32[8,2,8,8,64]{4,1,2,3,0:T(2,128)S(1)}, f32[8,2,8,8,64]{4,1,2,3,0:T(2,128)S(1)}) fusion(bf16[8,8,8,2,128]{4,3,2,1,0:T(2,128)(2,1)} %settle.1), kind=kLoop, calls=%fused_computation.44 | loop fusion | flops 131072 | bytes 786432 | tf_op jit(solution)/shard_map/convert_element_type | solution.py:595
  136.4 0.2 copy.168
  136.5 0.9 reshape.331
  137.4 0.2 copy.169
  137.6 0.9 reshape.332
  (59 shorter events, 1.8 us)
Async XLA Ops:
  0.6 2.0 %copy-start = (bf16[16,1024]{1,0:T(8,128)(2,1)S(1)}, bf16[16,1024]{1,0:T(8,128)(2,1)}, u32[]{:S(2)}) copy-start(bf16[16,1024]{1,0:T(8,128)(2,1)} %param.13) | copy-start | bytes 98308
  0.6 3.8 %copy-start.2 = (bf16[256,1024]{1,0:T(8,128)(2,1)S(1)}, bf16[256,1024]{1,0:T(8,128)(2,1)}, u32[]{:S(2)}) copy-start(bf16[256,1024]{1,0:T(8,128)(2,1)} %param.11) | copy-start | bytes 1572868
  0.7 3.5 %copy-start.4 = (bf16[256,1024]{1,0:T(8,128)(2,1)S(1)}, bf16[256,1024]{1,0:T(8,128)(2,1)}, u32[]{:S(2)}) copy-start(bf16[256,1024]{1,0:T(8,128)(2,1)} %param.12) | copy-start | bytes 1572868
  4.2 1.5 %copy-start.5 = (bf16[16,4096]{1,0:T(8,128)(2,1)S(1)}, bf16[16,4096]{1,0:T(8,128)(2,1)}, u32[]{:S(2)}) copy-start(bf16[16,4096]{1,0:T(8,128)(2,1)} %param.10) | copy-start | bytes 393220
  6.5 1.7 %copy-start.7 = (bf16[16,4096]{1,0:T(8,128)(2,1)S(1)}, bf16[16,4096]{1,0:T(8,128)(2,1)}, u32[]{:S(2)}) copy-start(bf16[16,4096]{1,0:T(8,128)(2,1)} %param.17) | copy-start | bytes 393220
  7.2 1.9 %copy-start.9 = (s32[16,1]{0,1:T(1,128)S(1)}, s32[16,1]{0,1:T(1,128)}, u32[]{:S(2)}) copy-start(s32[16,1]{0,1:T(1,128)} %param.16) | copy-start | bytes 196
  58.6 3.1 %copy-start.3 = (f32[8,16,128]{2,1,0:T(8,128)S(1)}, f32[8,16,128]{2,1,0:T(8,128)}, u32[]{:S(2)}) copy-start(f32[8,16,128]{2,1,0:T(8,128)} %get-tuple-element.12) | copy-start | bytes 196612
  60.2 2.2 %copy-start.6 = (bf16[8,8,16,256]{3,2,1,0:T(8,128)(2,1)S(1)}, bf16[8,8,16,256]{3,2,1,0:T(8,128)(2,1)}, u32[]{:S(2)}) copy-start(bf16[8,8,16,256]{3,2,1,0:T(8,128)(2,1)} %get-tuple-element.13) | copy-start | bytes 1572868
  62.5 1.6 %copy-start.1 = (bf16[8,8,8,16,128]{4,3,2,1,0:T(8,128)(2,1)S(1)}, bf16[8,8,8,16,128]{4,3,2,1,0:T(8,128)(2,1)}, u32[]{:S(2)}) copy-start(bf16[8,8,8,16,128]{4,3,2,1,0:T(8,128)(2,1)} %get-tuple-element.14) | copy-start | bytes 6291460
  104.4 1.0 copy-start.8
